TPU v7x, 256 devices: a whole 4x4x8 slice. The times are simulated.
256 devices in a mesh: depth: 64 (over z, y, core), tile: 4 (over x).
Axes of the slice: x: 4, y: 4, z: 8, core: 2. Of those that a mesh axis runs over, the one named last changes fastest.
Arguments:
- volume: bfloat16 [768, 4, 768, 512], P('depth', 'tile'), may hold values from -6 to 6
- table_index: int32 [768, 4, 768, 32], P('depth', 'tile'), may hold values from 0 to 15
- brick_position: int32 [64], replicated, may hold values from 0 to 63, each once
- tf_center: float32 [16], replicated, may hold values from -1.5 to 1.5
- tf_width: float32 [16], replicated, may hold values from 0.3 to 1.2
- tf_peak: float32 [16], replicated, may hold values from 2 to 32
- tf_color: float32 [3, 16], replicated, may hold values from 0.1 to 1
Outputs:
- frame: float32 [4, 4, 768, 512], P(None, 'tile', 'depth')
Inputs may be any that keep to these rules, and one draw needn't show every extreme that they name: `brick_position`: each depth rank has a different position.
All inputs are finite; a program needn't handle non-finite values.
Results may differ from a plain program's by a relative error of at most 0.0003.
Values may be sent and summed in bfloat16 or wider, within the bound.
No kernel may reach another device: no remote copies, remote signals or barrier semaphores. Data moves between devices by JAX's collectives and lax.ppermute only.
A program may use at most 128 MiB of HBM per device.

v0:
```python
import jax
import jax.numpy as jnp
from jax import lax
from jax.sharding import PartitionSpec as P

CELL = 16


def from_partner(value, axis, apart):
    return lax.ppermute(value, axis, [(i, i ^ 1 << apart) for i in range(lax.axis_size(axis))])


def light_sample(value, grad_x, grad_y, params, rgb, trans, inverse):
    energy = grad_x * grad_x + grad_y * grad_y
    facing = 0.6 * grad_x + 0.8 * grad_y
    shade = 0.3 + 0.7 * facing * facing / (1.0 + energy)
    scaled = (value - params[0]) / params[1]
    extinction = params[2] * jnp.exp(-0.5 * scaled * scaled) * energy * inverse
    keep = jnp.exp(-extinction)
    opacity = 1.0 - keep
    weight = trans * opacity
    rgb = rgb + weight[None] * params[3:6] * shade[None]
    trans = trans * keep
    return (rgb, trans)


def composite(layers):
    while layers.shape[1] > 1:
        front = layers[:, 0::2]
        back = layers[:, 1::2]
        layers = front + (1.0 - front[3:4]) * back
    return layers[:, 0]


def on_device(volume, table_index, brick_position, tf_center, tf_width, tf_peak, tf_color):
    tables = jnp.concatenate([tf_center[None], tf_width[None], tf_peak[None], tf_color], axis=0)
    samples = volume[:, 0]
    cells = table_index[:, 0]
    depth_count = samples.shape[0]
    height = samples.shape[1]
    width = samples.shape[2]
    cell_count = cells.shape[2]
    table_count = tables.shape[1]
    param_count = tables.shape[0]
    ranks = lax.axis_size("depth")
    inverse = 1.0 / (depth_count * ranks)
    tile_rank = lax.axis_index("tile")
    col_bit = tile_rank % 2
    row_bit = tile_rank // 2
    send_col = jnp.where(col_bit == 0, samples[:, :, width - 1], samples[:, :, 0])
    got_col = from_partner(send_col, "tile", 0)
    send_row = jnp.where(row_bit == 0, samples[:, height - 1, :], samples[:, 0, :])
    got_row = from_partner(send_row, "tile", 1)
    zero_col = jnp.zeros_like(got_col)
    zero_row = jnp.zeros_like(got_row)
    left_rim = jnp.where(col_bit == 1, got_col, zero_col)
    right_rim = jnp.where(col_bit == 0, got_col, zero_col)
    top_rim = jnp.where(row_bit == 1, got_row, zero_row)
    bottom_rim = jnp.where(row_bit == 0, got_row, zero_row)
    wide_pad = jnp.concatenate([left_rim[:, :, None], samples, right_rim[:, :, None]], axis=2)
    tall_pad = jnp.concatenate([top_rim[:, None, :], samples, bottom_rim[:, None, :]], axis=1)
    entries = jnp.arange(table_count, dtype=jnp.int32)
    table_grid = tables[:, :, None, None]

    def sample(step, carry):
        rgb, trans = carry
        wide = lax.dynamic_index_in_dim(wide_pad, step, 0, keepdims=False).astype(jnp.float32)
        tall = lax.dynamic_index_in_dim(tall_pad, step, 0, keepdims=False).astype(jnp.float32)
        cell_index = lax.dynamic_index_in_dim(cells, step, 0, keepdims=False)
        matches_cell = cell_index[None] == entries[:, None, None]
        cell_params = jnp.sum(jnp.where(matches_cell[None], table_grid, 0.0), axis=1)
        params = jnp.broadcast_to(cell_params[..., None], (param_count, height, cell_count, CELL))
        params = params.reshape(param_count, height, width)
        value = wide[:, 1:-1]
        grad_x = 0.5 * (wide[:, 2:] - wide[:, :-2])
        grad_y = 0.5 * (tall[2:, :] - tall[:-2, :])
        return light_sample(value, grad_x, grad_y, params, rgb, trans, inverse)

    start = (jnp.zeros((3, height, width), jnp.float32), jnp.ones((height, width), jnp.float32))
    rgb, trans = lax.fori_loop(0, depth_count, sample, start)
    partial_value = jnp.concatenate([rgb, (1.0 - trans)[None]], axis=0)
    piece_rows = height // ranks
    places = jnp.arange(ranks, dtype=jnp.int32)
    matches = brick_position[None, :] == places[:, None]
    rank_at = jnp.sum(jnp.where(matches, places[None, :], 0), axis=1)
    received = lax.all_to_all(partial_value, "depth", split_axis=1, concat_axis=0, tiled=True)
    stacked = received.reshape(ranks, 4, piece_rows, received.shape[2])
    ordered = jnp.take(stacked, rank_at, axis=0)
    image = composite(jnp.moveaxis(ordered, 0, 1))
    return image[:, None]


def solution(mesh):
    return jax.shard_map(
        on_device,
        mesh=mesh,
        in_specs=(
            P("depth", "tile", None, None),
            P("depth", "tile", None, None),
            P(),
            P(),
            P(),
            P(),
            P(),
        ),
        out_specs=P(None, "tile", "depth", None),
        check_vma=False,
    )
```

profile of v0, /device:TPU:4, one launch (start us, length us, event | category | flops | bytes accessed | tf_op | source)
XLA Modules:
  0.0 431.9 jit_solution(12411299759493671184)
XLA Ops:
  0.0 16.2 %copy.104 = bf16[12,1,768,512]{2,0,3,1:T(8,128)(2,1)} copy(bf16[12,1,768,512]{3,2,1,0:T(8,128)(2,1)} %param.9) | data formatting | bytes 18874368 | tf_op args[0]
  16.2 2.9 slice_select_fusion
  19.2 1.6 copy.105
  20.8 2.3 collective-permute-start.1
  24.3 2.0 collective-permute-done.1
  26.3 2.9 copy.106
  29.2 2.9 copy.107
  32.1 12.8 %pad_maximum_fusion = bf16[12,770,512]{1,0,2:T(8,128)(2,1)S(1)} fusion(bf16[12,1,512]{1,0,2:T(8,128)(2,1)} %copy.107, bf16[12,768,512]{1,0,2:T(8,128)(2,1)} %bitcast.100, bf16[12,1,512]{1,0,2:T(8,128)(2,1)} %copy.106), kind=kLoop, calls=%fused_computation.31 | loop fusion | flops 28385280 | bytes 18923520 | tf_op jit(solution)/shard_map/concatenate | solution.py:61
  45.0 5.4 %copy.109 = bf16[12,770,512]{1,2,0:T(8,128)(2,1)} copy(bf16[12,770,512]{1,0,2:T(8,128)(2,1)S(1)} %pad_maximum_fusion) | data formatting | bytes 18923520
  50.5 3.0 pad_maximum_fusion.1
  53.4 5.7 %copy.108 = bf16[12,768,514]{1,2,0:T(8,128)(2,1)} copy(bf16[12,768,514]{1,0,2:T(8,128)(2,1)S(1)} %pad_maximum_fusion.1) | data formatting | bytes 18948096
  59.1 133.1 %while.18 = (s32[]{:T(128)}, f32[3,768,512]{1,2,0:T(8,128)}, f32[768,512]{0,1:T(8,128)S(1)}, s32[12,768,32]{1,2,0:T(8,128)}, f32[6,16,1,1]{1,0,3,2:T(8,128)S(1)}...) while((s32[]{:T(128)}, f32[3,768,512]{1,2,0:T(8,128)}, ...), condition=%wide.region_3.4_spmd.clone, body=%wide.region_1.3_spmd.clone.sunk | while | flops 21481988 | bytes 75808312 | solution.py:80
  61.2 1.3 dynamic-slice_convert_fusion.2
  63.8 1.9 select_multiply_fusion.2
  66.1 1.8 fusion.24
  67.9 2.2 copy-done
  72.3 1.3 dynamic-slice_convert_fusion.2
  74.9 1.9 select_multiply_fusion.2
  77.2 1.8 fusion.24
  79.0 2.2 copy-done
  86.0 1.9 select_multiply_fusion.2
  88.3 1.8 fusion.24
  90.1 2.2 copy-done
  97.1 1.9 select_multiply_fusion.2
  99.3 1.8 fusion.24
  101.2 2.2 copy-done
  105.6 1.3 dynamic-slice_convert_fusion.2
  108.2 1.9 select_multiply_fusion.2
  110.4 1.8 fusion.24
  112.3 2.2 copy-done
  116.7 1.3 dynamic-slice_convert_fusion.2
  119.2 1.9 select_multiply_fusion.2
  121.5 1.8 fusion.24
  123.4 2.2 copy-done
  130.3 1.9 select_multiply_fusion.2
  132.6 1.8 fusion.24
  134.5 2.2 copy-done
  141.4 1.9 select_multiply_fusion.2
  143.7 1.8 fusion.24
  145.5 2.2 copy-done
  152.5 1.9 select_multiply_fusion.2
  154.8 1.8 fusion.24
  156.6 2.2 copy-done
  163.6 1.9 select_multiply_fusion.2
  165.9 1.8 fusion.24
  167.7 2.2 copy-done
  174.7 1.9 select_multiply_fusion.2
  177.0 1.8 fusion.24
  178.8 2.2 copy-done
  185.8 1.9 select_multiply_fusion.2
  188.1 1.8 fusion.24
  189.9 2.2 copy-done
  192.2 7.3 %copy.111 = f32[3,768,512]{2,0,1:T(4,128)} copy(f32[3,768,512]{1,2,0:T(8,128)} %get-tuple-element.205) | data formatting | bytes 9437184 | tf_op jit(solution)/shard_map/while | solution.py:80
  201.2 8.3 %pad_maximum_fusion.2 = f32[4,768,512]{2,0,1:T(4,128)} fusion(f32[1,768,512]{2,0,1:T(1,128)S(1)} %broadcast_in_dim.173, f32[3,768,512]{2,0,1:T(4,128)} %copy.111), kind=kLoop, calls=%fused_computation.33 | loop fusion | flops 1572864 | bytes 12582912 | tf_op jit(solution)/shard_map/concatenate | solution.py:81
  209.5 12.5 %all-to-all-start = ((f32[4,768,512]{2,0,1:T(4,128)}), f32[4,768,512]{2,0,1:T(4,128)}, u32[]{:S(2)}, u32[]{:S(2)}) async-start(f32[4,768,512]{2,0,1:T(4,128)} %pad_maximum_fusion.2), calls=%async_computation | async-start | bytes 12582912 | tf_op jit(solution)/shard_map/all_to_all | solution.py:86
  222.1 141.1 %all-to-all-done = f32[4,768,512]{2,0,1:T(4,128)} async-done(((f32[4,768,512]{2,0,1:T(4,128)}), f32[4,768,512]{2,0,1:T(4,128)}, u32[]{:S(2)}, u32[]{:S(2)}) %all-to-all-start) | async-done | bytes 6291488 | tf_op jit(solution)/shard_map/all_to_all | solution.py:86
  363.3 9.3 %gather_fusion = f32[64,4,12,512]{3,1,2,0:T(4,128)} fusion(f32[64,4,12,512]{3,1,2,0:T(4,128)} %bitcast.13, s32[1024]{0:T(1024)S(1)} %pad_clamp_fusion), kind=kCustom, calls=%fused_computation | custom fusion | bytes 12583168 | tf_op jit(solution)/shard_map/jit(_take)/gather | solution.py:88
  372.6 9.5 %fusion.13 = f32[4,64,12,512]{3,1,2,0:T(8,128)} fusion(f32[64,4,12,512]{3,1,2,0:T(4,128)} %gather_fusion, pred[64]{0:T(512)(128)(4,1)S(1)} %compare_and_fusion), kind=kLoop, calls=%fused_computation.35 | loop fusion | flops 1572864 | bytes 12582976 | tf_op jit(solution)/shard_map/jit(_take)/select_n | solution.py:88
  382.1 12.1 %slice.181 = f32[4,32,12,512]{3,1,2,0:T(8,128)S(1)} slice(f32[4,64,12,512]{3,1,2,0:T(8,128)} %fusion.13), slice={[0:4:1], [0:64:2], [0:12:1], [0:512:1]} | slice | bytes 6291456 | tf_op jit(solution)/shard_map/slice | solution.py:29
  394.2 14.2 %slice.183 = f32[4,32,12,512]{3,1,2,0:T(8,128)} slice(f32[4,64,12,512]{3,1,2,0:T(8,128)} %fusion.13), slice={[0:4:1], [1:64:2], [0:12:1], [0:512:1]} | slice | bytes 6291456 | tf_op jit(solution)/shard_map/slice | solution.py:30
  408.4 4.5 %multiply_add_fusion = f32[4,32,12,512]{3,1,2,0:T(8,128)} fusion(f32[4,32,12,512]{3,1,2,0:T(8,128)S(1)} %slice.181, f32[4,32,12,512]{3,1,2,0:T(8,128)} %slice.183, f32[32,12,512]{2,0,1:T(8,128)S(1)} %fusion.14), kind=kLoop, calls=%fused_computation.36 | loop fusion | flops 1572864 | bytes 10223616 | tf_op jit(solution)/shard_map/add | solution.py:31
  412.9 7.8 %slice.184 = f32[4,16,12,512]{3,1,2,0:T(8,128)} slice(f32[4,32,12,512]{3,1,2,0:T(8,128)} %multiply_add_fusion), slice={[0:4:1], [0:32:2], [0:12:1], [0:512:1]} | slice | bytes 3145728 | tf_op jit(solution)/shard_map/slice | solution.py:29
  420.7 4.2 slice.186
  425.9 2.3 multiply_add_fusion.1
  (227 shorter events, 63.8 us)
Async XLA Ops:
  19.1 5.1 %copy-start.2 = (f32[3,16]{1,0:T(4,128)S(1)}, f32[3,16]{1,0:T(4,128)}, u32[]{:S(2)}) copy-start(f32[3,16]{1,0:T(4,128)} %param.15) | copy-start | bytes 580
  19.1 5.1 %copy-start.3 = (f32[16]{0:T(128)S(1)}, f32[16]{0:T(128)}, u32[]{:S(2)}) copy-start(f32[16]{0:T(128)} %param.14) | copy-start | bytes 196
  19.1 5.1 %copy-start.4 = (f32[16]{0:T(128)S(1)}, f32[16]{0:T(128)}, u32[]{:S(2)}) copy-start(f32[16]{0:T(128)} %param.13) | copy-start | bytes 196
  19.1 5.1 %copy-start.5 = (f32[16]{0:T(128)S(1)}, f32[16]{0:T(128)}, u32[]{:S(2)}) copy-start(f32[16]{0:T(128)} %param.12) | copy-start | bytes 196
  20.8 5.5 %collective-permute-start.1 = (bf16[12,512]{1,0:T(8,128)(2,1)S(1)}, bf16[12,512]{1,0:T(8,128)(2,1)S(1)}, u32[]{:S(2)}, u32[]{:S(2)}) collective-permute-start(bf16[12,512]{1,0:T(8,128)(2,1)S(1)} %bitcast.117), channel_id=1, source_target_pairs={{0,2},{1,3},{2,0},{3,1},{4,6},{5,7},{6,4},{7,5},{8,10},{9,11},{10,... | collective-permute-start | bytes 36872 | tf_op jit(solution)/shard_map/ppermute | solution.py:10
  23.9 26.5 %collective-permute-start = (bf16[12,768]{1,0:T(8,128)(2,1)S(1)}, bf16[12,768]{1,0:T(8,128)(2,1)S(1)}, u32[]{:S(2)}, u32[]{:S(2)}) collective-permute-start(bf16[12,768]{1,0:T(8,128)(2,1)S(1)} %fusion.20), channel_id=1, source_target_pairs={{0,1},{1,0},{2,3},{3,2},{4,5},{5,4},{6,7},{7,6},{8,9},{9,8},{10,11... | collective-permute-start | bytes 55304 | tf_op jit(solution)/shard_map/ppermute | solution.py:10
  32.1 18.3 %slice-start.2 = ((s8[12582912]{0:T(1024)(128)(4,1)}), s8[4194304]{0:T(1024)(128)(4,1)S(1)}, s32[]{:S(2)}) async-start(s8[12582912]{0:T(1024)(128)(4,1)} %bitcast.101), calls=%async_computation.3 | async-start | bytes 8388608
  32.1 18.3 %slice-start.3 = ((s8[12582912]{0:T(1024)(128)(4,1)}), s8[4194304]{0:T(1024)(128)(4,1)S(1)}, s32[]{:S(2)}) async-start(s8[12582912]{0:T(1024)(128)(4,1)} %bitcast.101), calls=%async_computation.4 | async-start | bytes 8388608
  45.0 5.5 %slice-start.4 = ((s8[12582912]{0:T(1024)(128)(4,1)}), s8[4194304]{0:T(1024)(128)(4,1)S(1)}, s32[]{:S(2)}) async-start(s8[12582912]{0:T(1024)(128)(4,1)} %bitcast.101), calls=%async_computation.5 | async-start | bytes 8388608
  63.8 2.2 slice-start
  63.8 2.3 slice-start.1
  67.9 2.2 copy-start
  74.9 2.2 slice-start
  74.9 2.3 slice-start.1
  79.0 2.2 copy-start
  85.9 2.2 slice-start
  86.0 2.3 slice-start.1
  90.1 2.2 copy-start
  97.0 2.2 slice-start
  97.1 2.3 slice-start.1
  101.2 2.2 copy-start
  108.1 2.2 slice-start
  108.1 2.3 slice-start.1
  112.3 2.2 copy-start
  119.2 2.2 slice-start
  119.2 2.3 slice-start.1
  123.3 2.2 copy-start
  130.3 2.2 slice-start
  130.3 2.3 slice-start.1
  134.4 2.2 copy-start
  141.4 2.2 slice-start
  141.4 2.3 slice-start.1
  145.5 2.2 copy-start
  152.5 2.2 slice-start
  152.5 2.3 slice-start.1
  156.6 2.2 copy-start
  163.6 2.2 slice-start
  163.6 2.3 slice-start.1
  167.7 2.2 copy-start
  174.7 2.2 slice-start
  174.7 2.3 slice-start.1
  178.8 2.2 copy-start
  185.8 2.2 slice-start
  185.8 2.3 slice-start.1
  189.9 2.2 copy-start
  209.5 12.5 %copy-start.6 = (s32[64]{0:T(128)S(1)}, s32[64]{0:T(128)}, u32[]{:S(2)}) copy-start(s32[64]{0:T(128)} %param.11) | copy-start | bytes 772
  209.5 153.8 %all-to-all-start = ((f32[4,768,512]{2,0,1:T(4,128)}), f32[4,768,512]{2,0,1:T(4,128)}, u32[]{:S(2)}, u32[]{:S(2)}) async-start(f32[4,768,512]{2,0,1:T(4,128)} %pad_maximum_fusion.2), calls=%async_computation | async-start | bytes 12582912 | tf_op jit(solution)/shard_map/all_to_all | solution.py:86
  412.9 7.8 %copy-start.1 = (f32[4,32,12,512]{3,1,2,0:T(8,128)S(1)}, f32[4,32,12,512]{3,1,2,0:T(8,128)}, u32[]{:S(2)}) copy-start(f32[4,32,12,512]{3,1,2,0:T(8,128)} %multiply_add_fusion) | copy-start | bytes 9437188
where the time goes:
time: 435 us; the launch traced here: 432 us
  waiting for transfers between devices  143 us (33%)
  other arithmetic  139 us (32%)
  local copies, waits for them, and re-layouts  133 us (31%)
  starting transfers between devices  15.2 us (3%)
    all_to_all x1, waiting for transfers between devices, on_device(): lax.all_to_all(partial_value, 'depth', split_axis=1, concat_axis=0, tiled...  141 us
    while x84, local copies, waits for them, and re-layouts  28.4 us
    unnamed x22, local copies, waits for them, and re-layouts  27.4 us
    mul x12, other arithmetic, light_sample(): trans = trans * keep  22.4 us
    add x12, other arithmetic, light_sample(): rgb = rgb + weight[None] * params[3:6] * shade[None]  21.8 us
    slice x5, local copies, waits for them, and re-layouts, composite(): front = layers[:, 0::2]  21.1 us
    slice x5, local copies, waits for them, and re-layouts, composite(): back = layers[:, 1::2]  19.6 us
    convert_element_type x12, other arithmetic, sample(): lax.dynamic_index_in_dim(tall_pad, step, 0, keepdims=False)  15.7 us
  transfers between devices with their start and end apart: 3, of which 2 were waited for; matrix products, arithmetic and copies ran while one was open for 6% of the time, Pallas kernels for 0%

commit v1 on v0

v1 whole, which is shorter than its diff:
```python
import functools

import jax
import jax.numpy as jnp
from jax import lax
from jax.experimental import pallas as pl
from jax.experimental.pallas import tpu as pltpu
from jax.sharding import PartitionSpec as P

CELL = 16
LANES = 128
SIDE = 8
BAND = 256
LOG2E = 1.4426950408889634
LEVELS = 65535.0
CHUNKS = ((1,), (0, 2, 3))
STEP_SAMPLES = 3

NT = (((1,), (1,)), ((), ()))
NN = (((1,), (0,)), ((), ()))


def from_partner(value, axis, apart):
    return lax.ppermute(value, axis, [(i, i ^ 1 << apart) for i in range(lax.axis_size(axis))])


def tile_of(tiles, j):
    tile = jnp.int32(tiles[0])
    for n in range(1, len(tiles)):
        tile = jnp.where(j == n, jnp.int32(tiles[n]), tile)
    return tile


def code(value):
    root = lax.rsqrt(lax.rsqrt(jnp.maximum(value, 0.0)))
    return jnp.minimum(root * LEVELS + 0.5, LEVELS).astype(jnp.int32)


def decode(word):
    root = word.astype(jnp.float32) * (1.0 / LEVELS)
    square = root * root
    return square * square


def march_kernel(tiles, sizes, *refs):
    steps, height, width, total = sizes
    (center_ref, wide_ref, peak_ref, color_ref, vol_ref, rim_row_ref, index_ref, rim_col_ref) = refs[:8]
    if rim_col_ref is None:
        out_ref, edge_ref = refs[8:10]
        scratch = refs[10:]
    else:
        out_ref = refs[8]
        edge_ref = None
        scratch = refs[9:]
    (pick_ref, band_ref, ends_ref, table_ref, value_ref, grad_ref, param_ref, pair_a, pair_b, turn_a, turn_b) = scratch
    j = pl.program_id(0)
    part = pl.program_id(1)
    tile = tile_of(tiles, j)
    span = LANES + 2 * SIDE

    @pl.when(part == 0)
    def _():
        row = lax.broadcasted_iota(jnp.int32, (span, width), 0)
        col = lax.broadcasted_iota(jnp.int32, (span, width), 1)
        want = tile * LANES + row - SIDE
        want = jnp.where(row == 0, 0, jnp.where(row == 1, width - 1, want))
        pick_ref[...] = jnp.where(col == want, 1.0, 0.0).astype(jnp.bfloat16)

    @pl.when((part == 0) & (j == 0))
    def _():
        k = lax.broadcasted_iota(jnp.int32, (BAND, BAND), 0)
        r = lax.broadcasted_iota(jnp.int32, (BAND, BAND), 1)
        band = jnp.where(k == r + 1, 1.0, jnp.where(k == r - 1, -1.0, 0.0))
        band_ref[...] = band.astype(jnp.bfloat16)
        k = lax.broadcasted_iota(jnp.int32, (16, BAND), 0)
        r = lax.broadcasted_iota(jnp.int32, (16, BAND), 1)
        for n in range(height // BAND):
            above = (k == 2 * n) & (r == 0)
            below = (k == 2 * n + 1) & (r == BAND - 1)
            ends_ref[n] = jnp.where(below, 1.0, jnp.where(above, -1.0, 0.0)).astype(jnp.bfloat16)
        shape = (8, 16)
        scale = (0.5 * LOG2E) ** 0.5 / wide_ref[...]
        table_ref[0, :, 0:16] = jnp.broadcast_to(center_ref[...], shape)
        table_ref[1, :, 0:16] = jnp.broadcast_to(scale, shape)
        table_ref[2, :, 0:16] = jnp.broadcast_to(jnp.log2(peak_ref[...] * (0.25 * LOG2E / total)), shape)
        for n in range(3):
            table_ref[3 + n, :, 0:16] = jnp.broadcast_to(color_ref[n : n + 1, :], shape)

    pick = pick_ref[...]
    inner = pick[SIDE : SIDE + LANES]
    for q in range(STEP_SAMPLES):
        s = part * STEP_SAMPLES + q
        rims = lax.dot_general(inner, rim_row_ref[q], NT, preferred_element_type=jnp.float32).astype(jnp.bfloat16)
        for n in range(height // BAND):
            rows = slice(BAND * n, BAND * n + BAND)
            turned = lax.dot_general(pick, vol_ref[q, rows, :], NT, preferred_element_type=jnp.float32)
            for m in range(BAND // LANES):
                value_ref[s, 2 * n + m] = turned[:, LANES * m : LANES * m + LANES]
            short = turned[SIDE : SIDE + LANES].astype(jnp.bfloat16)
            grad = lax.dot_general(short, band_ref[...], NN, preferred_element_type=jnp.float32)
            grad = grad + lax.dot_general(rims, ends_ref[n], NN, preferred_element_type=jnp.float32)
            for m in range(BAND // LANES):
                grad_ref[s, 2 * n + m] = grad[:, LANES * m : LANES * m + LANES]
        if edge_ref is not None:
            for n in range(height // LANES):
                edge_ref[q, :, LANES * n : LANES * n + LANES] = value_ref[s, n, 0:SIDE, :]
        if rim_col_ref is not None:

            @pl.when(tile == 0)
            def _():
                for n in range(height // LANES):
                    value_ref[s, n, SIDE - 1 : SIDE, :] = rim_col_ref[q, 0:1, LANES * n : LANES * n + LANES]

            @pl.when(tile == width // LANES - 1)
            def _():
                for n in range(height // LANES):
                    value_ref[s, n, SIDE + LANES : SIDE + LANES + 1, :] = rim_col_ref[q, 1:2, LANES * n : LANES * n + LANES]

        for n in range(height // LANES):
            lanes = slice(LANES * n, LANES * n + LANES)
            index = index_ref[q, :, lanes]
            for p in range(6):
                param_ref[s, p, n] = jnp.take_along_axis(table_ref[p], index, axis=1)

    @pl.when(part == steps // STEP_SAMPLES - 1)
    def _():
        groups = LANES // CELL

        def strip(i, carry):
            g = i % groups
            lane = i // groups
            base = pl.multiple_of(g * CELL, CELL)
            zero = jnp.zeros((8, LANES), jnp.float32)
            state = [[zero, zero + 1.0, zero, zero, zero] for _ in range(2)]
            for s in range(steps):
                param = [param_ref[s, p, lane, pl.ds(g, 8, stride=0), :] for p in range(6)]
                for u in range(2):
                    depth, trans, red, green, blue = state[u]
                    at = base + 8 * u
                    value = value_ref[s, lane, pl.ds(at + SIDE, 8), :]
                    ahead = value_ref[s, lane, pl.ds(at + SIDE + 1, 8), :]
                    behind = value_ref[s, lane, pl.ds(at + SIDE - 1, 8), :]
                    grad_x = ahead - behind
                    grad_y = grad_ref[s, lane, pl.ds(at, 8), :]
                    energy = grad_x * grad_x + grad_y * grad_y
                    facing = 0.6 * grad_x + 0.8 * grad_y
                    shade = 0.3 + 0.7 * (facing * facing / (4.0 + energy))
                    scaled = (value - param[0]) * param[1]
                    rate = jnp.exp2(param[2] - scaled * scaled)
                    depth = depth - rate * energy
                    after = jnp.exp2(depth)
                    weight = (trans - after) * shade
                    red = red + weight * param[3]
                    green = green + weight * param[4]
                    blue = blue + weight * param[5]
                    state[u] = [depth, after, red, green, blue]
            for u in range(2):
                depth, trans, red, green, blue = state[u]
                at = pl.ds(base + 8 * u, 8)
                pair_a[lane, at, :] = (code(red) << 16) | code(green)
                pair_b[lane, at, :] = (code(blue) << 16) | code(1.0 - trans)
            return carry

        lax.fori_loop(0, groups * (height // LANES), strip, 0)
        for n in range(height // LANES):
            lanes = slice(LANES * n, LANES * n + LANES)
            turn_a[lanes, :] = pair_a[n].T
            turn_b[lanes, :] = pair_b[n].T

        def pack(d, carry):
            for u in range(4):
                e = d * 4 + u
                r = e * 12
                out_ref[e, 0:8, :] = turn_a[pl.ds(r, 8), :]
                out_ref[e, 8:12, :] = turn_a[pl.ds(r + 8, 4), :]
                out_ref[e, 12:16, :] = turn_b[pl.ds(r + 8, 4), :]
                out_ref[e, 16:24, :] = turn_b[pl.ds(r, 8), :]
            return carry

        lax.fori_loop(0, out_ref.shape[0] // 4, pack, 0)


def march(tiles, ranks, tables, samples, rim_rows, cells, rim_cols):
    steps, height, width = samples.shape
    ahead = rim_cols is None
    span = LANES + 2 * SIDE
    batch = STEP_SAMPLES
    sizes = (steps, height, width, steps * ranks)

    def body(*refs):
        refs = list(refs)
        if ahead:
            refs.insert(7, None)
        march_kernel(tiles, sizes, *refs)

    small = lambda shape: pl.BlockSpec(shape, lambda j, s: (0, 0))
    in_specs = [small((1, 16)), small((1, 16)), small((1, 16)), small((3, 16))]
    in_specs += [
        pl.BlockSpec((batch, height, width), lambda j, s: (s, 0, 0)),
        pl.BlockSpec((batch, 16, width), lambda j, s: (s, 0, 0)),
        pl.BlockSpec((batch, LANES // CELL, height), lambda j, s: (s, tile_of(tiles, j), 0)),
    ]
    piece = height // ranks
    out_shape = [jax.ShapeDtypeStruct((ranks, 2 * piece, LANES * len(tiles)), jnp.int32)]
    out_specs = [pl.BlockSpec((ranks, 2 * piece, LANES), lambda j, s: (0, 0, j))]
    args = list(tables) + [samples, rim_rows, cells]
    if ahead:
        out_shape.append(jax.ShapeDtypeStruct((steps, SIDE, height), jnp.float32))
        out_specs.append(pl.BlockSpec((batch, SIDE, height), lambda j, s: (s, 0, 0)))
    else:
        in_specs.append(pl.BlockSpec((batch, 2, height), lambda j, s: (s, 0, 0)))
        args.append(rim_cols)
    points = steps * height * LANES * len(tiles)
    return pl.pallas_call(
        body,
        grid=(len(tiles), steps // batch),
        in_specs=in_specs,
        out_specs=out_specs,
        out_shape=out_shape,
        scratch_shapes=[
            pltpu.VMEM((span, width), jnp.bfloat16),
            pltpu.VMEM((BAND, BAND), jnp.bfloat16),
            pltpu.VMEM((height // BAND, 16, BAND), jnp.bfloat16),
            pltpu.VMEM((6, 8, LANES), jnp.float32),
            pltpu.VMEM((steps, height // LANES, span, LANES), jnp.float32),
            pltpu.VMEM((steps, height // LANES, LANES, LANES), jnp.float32),
            pltpu.VMEM((steps, 6, height // LANES, LANES // CELL, LANES), jnp.float32),
            pltpu.VMEM((height // LANES, LANES, LANES), jnp.int32),
            pltpu.VMEM((height // LANES, LANES, LANES), jnp.int32),
            pltpu.VMEM((height, LANES), jnp.int32),
            pltpu.VMEM((height, LANES), jnp.int32),
        ],
        compiler_params=pltpu.CompilerParams(
            dimension_semantics=("arbitrary", "arbitrary"), vmem_limit_bytes=56 * 1024 * 1024
        ),
        cost_estimate=pl.CostEstimate(flops=40 * points, bytes_accessed=2 * points, transcendentals=3 * points),
        name="march",
    )(*args)


def blend_kernel(tiles, place_ref, got_ref, *refs):
    out_ref, rank_ref = refs[-2:]
    ranks = got_ref.shape[0]

    def note(d, carry):
        rank_ref[place_ref[d]] = d
        return carry

    lax.fori_loop(0, ranks, note, 0)
    count = len(tiles)
    lower = lax.broadcasted_iota(jnp.int32, (8, LANES), 0) < 4
    zero = jnp.zeros((8, LANES), jnp.float32)
    one = zero + 1.0

    def layer(i, carry):
        carry = list(carry)
        for u in range(2):
            d = rank_ref[i * 2 + u]
            for n in range(count):
                lanes = slice(LANES * n, LANES * n + LANES)
                red, green, blue, alpha, trans, high, low, half = carry[n]
                first = got_ref[d, 0:8, lanes]
                mixed = got_ref[d, 8:16, lanes]
                last = got_ref[d, 16:24, lanes]
                cover = decode(last & 0xFFFF) * trans
                red = red + trans * decode(lax.shift_right_logical(first, 16))
                green = green + trans * decode(first & 0xFFFF)
                blue = blue + trans * decode(lax.shift_right_logical(last, 16))
                alpha = alpha + cover
                trans = trans - cover
                level = decode(mixed & 0xFFFF)
                opaque = jnp.where(lower, pltpu.roll(level, 4, 0), level)
                high = high + half * decode(lax.shift_right_logical(mixed, 16))
                low = low + half * level
                half = half - half * opaque
                carry[n] = (red, green, blue, alpha, trans, high, low, half)
        return tuple(carry)

    start = tuple((zero, zero, zero, zero, one, zero, zero, one) for _ in range(count))
    final = lax.fori_loop(0, ranks // 2, layer, start)
    for n in range(count):
        lanes = slice(LANES * tiles[n], LANES * tiles[n] + LANES)
        red, green, blue, alpha, trans, high, low, half = final[n]
        out_ref[0, 0:8, lanes] = red
        out_ref[1, 0:8, lanes] = green
        out_ref[2, 0:8, lanes] = blue
        out_ref[3, 0:8, lanes] = alpha
        out_ref[0, 8:12, lanes] = high[0:4]
        out_ref[1, 8:12, lanes] = low[0:4]
        out_ref[2, 8:12, lanes] = high[4:8]
        out_ref[3, 8:12, lanes] = low[4:8]


def blend(tiles, brick_position, got, image, width):
    ranks, rows, lanes = got.shape
    piece = rows // 2
    whole = pl.BlockSpec(memory_space=pltpu.VMEM)
    in_specs = [pl.BlockSpec(memory_space=pltpu.SMEM), whole]
    args = [brick_position, got]
    body = functools.partial(blend_kernel, tiles)
    if image is not None:
        inner = body

        def body(place_ref, got_ref, image_ref, out_ref, rank_ref):
            out_ref[...] = image_ref[...]
            inner(place_ref, got_ref, out_ref, rank_ref)

        in_specs.append(whole)
        args.append(image)
    return pl.pallas_call(
        body,
        in_specs=in_specs,
        out_specs=whole,
        out_shape=jax.ShapeDtypeStruct((4, piece, width), jnp.float32),
        scratch_shapes=[pltpu.SMEM((ranks,), jnp.int32)],
        cost_estimate=pl.CostEstimate(flops=40 * got.size, bytes_accessed=4 * got.size, transcendentals=0),
        name="blend",
    )(*args)


def on_device(volume, table_index, brick_position, tf_center, tf_width, tf_peak, tf_color):
    samples = volume[:, 0]
    cells = jnp.swapaxes(table_index[:, 0], 1, 2)
    height = samples.shape[1]
    width = samples.shape[2]
    ranks = lax.axis_size("depth")
    tables = [tf_center[None], tf_width[None], tf_peak[None], tf_color]
    tile_rank = lax.axis_index("tile")
    col_bit = tile_rank % 2
    row_bit = tile_rank // 2
    send_row = jnp.where(row_bit == 0, samples[:, height - 1, :], samples[:, 0, :])
    got_row = from_partner(send_row, "tile", 1)
    zero_row = jnp.zeros_like(got_row)
    ends = [jnp.where(row_bit == 1, got_row, zero_row)]
    for n in range(1, height // BAND):
        ends += [samples[:, BAND * n, :], samples[:, BAND * n - 1, :]]
    ends += [jnp.where(row_bit == 0, got_row, zero_row)]
    rim_rows = jnp.stack(ends, axis=1)
    rim_rows = jnp.pad(rim_rows, ((0, 0), (0, 16 - len(ends)), (0, 0)))
    early, edges = march(CHUNKS[0], ranks, tables, samples, rim_rows, cells, None)
    swap = functools.partial(lax.all_to_all, axis_name="depth", split_axis=0, concat_axis=0, tiled=True)
    got_early = swap(early)
    send_col = jnp.where(col_bit == 0, edges[:, 1], edges[:, 0]).astype(jnp.bfloat16)
    got_col = from_partner(send_col, "tile", 0).astype(jnp.float32)
    zero_col = jnp.zeros_like(got_col)
    rim_cols = jnp.stack([jnp.where(col_bit == 1, got_col, zero_col), jnp.where(col_bit == 0, got_col, zero_col)], axis=1)
    (late,) = march(CHUNKS[1], ranks, tables, samples, rim_rows, cells, rim_cols)
    got_late = swap(late)
    image = blend(CHUNKS[0], brick_position, got_early, None, width)
    image = blend(CHUNKS[1], brick_position, got_late, image, width)
    return image[:, None]


def solution(mesh):
    return jax.shard_map(
        on_device,
        mesh=mesh,
        in_specs=(
            P("depth", "tile", None, None),
            P("depth", "tile", None, None),
            P(),
            P(),
            P(),
            P(),
            P(),
        ),
        out_specs=P(None, "tile", "depth", None),
        check_vma=False,
    )
```

time: 435 us -> 182 us (0.42)
  other arithmetic: 139 us -> 1.98 us
  local copies, waits for them, and re-layouts: 133 us -> 6.01 us
  Pallas kernels: 0 us -> 87.8 us
  waiting for transfers between devices: 143 us -> 59.5 us
  starting transfers between devices: 15.2 us -> 26 us
    pallas_call x0 -> x4, Pallas kernels: none -> 87.8 us  [the longest x2 80.3 us: march(): pl.pallas_call(body, grid=(len(tiles), steps // batch), in_specs=in_specs...]
    all_to_all x1 -> x2, waiting for transfers between devices: 141 us -> 53.9 us  [the longest x1 53.9 us: on_device(): got_late = swap(late)]
    slice x34 -> x0, local copies, waits for them, and re-layouts: 41.2 us -> none  [the longest x5 21.1 us: composite(): front = layers[:, 0::2]]
    while x86 -> x0, local copies, waits for them, and re-layouts: 36.1 us -> none
    convert_element_type x24 -> x1, other arithmetic: 30.8 us -> 0.01 us  [on_device(): jnp.where(col_bit == 0, edges[:, 1], edges[:, 0]).astype(jnp.bfloat16)]
    add x18 -> x0, other arithmetic: 29.6 us -> none  [the longest x12 21.8 us: light_sample(): rgb = rgb + weight[None] * params[3:6] * shade[None]]
    mul x29 -> x0, other arithmetic: 27.4 us -> none  [the longest x12 22.4 us: light_sample(): trans = trans * keep]
    unnamed x22 -> x5, local copies, waits for them, and re-layouts: 27.4 us -> 2.29 us
  transfers between devices with their start and end apart: 3 -> 4, of which waited for: 2 -> 3; matrix products, arithmetic and copies ran while one was open for 6% -> 1% of each run, Pallas kernels for 0% -> 35%
where the time goes in v1:
time: 182 us; the launch traced here: 181 us
  Pallas kernels  87.8 us (48%)
  waiting for transfers between devices  59.5 us (33%)
  starting transfers between devices  26 us (14%)
  local copies, waits for them, and re-layouts  6.01 us (3%)
  other arithmetic  1.98 us (1%)
    pallas_call x2, Pallas kernels, march(): pl.pallas_call(body, grid=(len(tiles), steps // batch), in_specs=in_specs...  80.3 us
    all_to_all x1, waiting for transfers between devices, on_device(): got_late = swap(late)  53.9 us
    all_to_all x1, starting transfers between devices, on_device(): got_early = swap(early)  12.1 us
    all_to_all x1, starting transfers between devices, on_device(): got_late = swap(late)  10.3 us
    pallas_call x2, Pallas kernels, blend(): pl.pallas_call(body, in_specs=in_specs, out_specs=whole, out_shape=jax.Sh...  7.51 us
    ppermute x2, waiting for transfers between devices, from_partner(): lax.ppermute(value, axis, [(i, i ^ 1 << apart) for i in range(lax.axis_si...  5.66 us
  transfers between devices with their start and end apart: 4, of which 3 were waited for; matrix products, arithmetic and copies ran while one was open for 1% of the time, Pallas kernels for 35%

profile of v1, /device:TPU:4, one launch (start us, length us, event | category | flops | bytes accessed | tf_op | source)
XLA Modules:
  0.0 181.4 jit_solution(2802152550310242850)
XLA Ops:
  0.0 1.3 fusion.3
  1.3 2.3 %collective-permute-start = (bf16[12,512]{1,0:T(8,128)(2,1)S(1)}, bf16[12,512]{1,0:T(8,128)(2,1)S(1)}, u32[]{:S(2)}, u32[]{:S(2)}) collective-permute-start(bf16[12,512]{1,0:T(8,128)(2,1)S(1)} %bitcast.25), channel_id=1, source_target_pairs={{0,2},{1,3},{2,0},{3,1},{4,6},{5,7},{6,4},{7,5},{8,10},{9,11},{10,... | collective-permute-start | bytes 36872 | tf_op jit(solution)/shard_map/ppermute | solution.py:24
  3.6 3.0 %collective-permute-done = bf16[12,512]{1,0:T(8,128)(2,1)S(1)} collective-permute-done((bf16[12,512]{1,0:T(8,128)(2,1)S(1)}, bf16[12,512]{1,0:T(8,128)(2,1)S(1)}, u32[]{:S(2)}, u32[]{:S(2)}) %collective-permute-start) | collective-permute-done | bytes 12320 | tf_op jit(solution)/shard_map/ppermute | solution.py:24
  6.7 0.2 stack.20
  6.9 0.7 pad.4.refs_5_
  7.6 19.9 %march.2 = (s32[64,24,128]{2,1,0:T(8,128)}, f32[12,8,768]{2,1,0:T(8,128)}) custom-call(f32[1,16]{1,0:T(1,128)} %bitcast.26, f32[1,16]{1,0:T(1,128)} %bitcast.28, f32[1,16]{1,0:T(1,128)} %bitcast.30, f32[3,16]{1,0:T(4,128)} %refs_3_.3, bf16[12,768,512]{2,1,0:T(8,128)(2,1)} %bitcast.20, bf16[12,16,512]{2,1,0:T(8,128)(2,1)} %pad.4.refs_5_, s32[12,32,768]{2,1,0:T(8,128)} %bitcast.22), custom_call_target="tpu_custom_call" | custom-call | flops 47185920 | bytes 2359296 | tf_op jit(solution)/shard_map/march/pallas_call | solution.py:214
  27.5 12.1 %all-to-all-start.1 = ((s32[64,24,128]{2,1,0:T(8,128)}), s32[64,24,128]{2,1,0:T(8,128)S(1)}, u32[]{:S(2)}, u32[]{:S(2)}) async-start(s32[64,24,128]{2,1,0:T(8,128)} %get-tuple-element.8), calls=%async_computation.1 | async-start | bytes 1572864 | tf_op jit(solution)/shard_map/all_to_all | solution.py:342
  39.6 1.0 copy.33
  40.7 1.3 collective-permute-start.1
  42.0 2.6 %collective-permute-done.1 = bf16[12,768]{1,0:T(8,128)(2,1)S(1)} collective-permute-done((bf16[12,768]{1,0:T(8,128)(2,1)S(1)}, bf16[12,768]{1,0:T(8,128)(2,1)S(1)}, u32[]{:S(2)}, u32[]{:S(2)}) %collective-permute-start.1) | collective-permute-done | bytes 18464 | tf_op jit(solution)/shard_map/ppermute | solution.py:24
  44.7 0.7 pad_maximum_fusion.refs_7_
  45.4 60.4 %march.3 = s32[64,24,384]{2,1,0:T(8,128)} custom-call(f32[1,16]{1,0:T(1,128)} %bitcast.27, f32[1,16]{1,0:T(1,128)} %bitcast.29, f32[1,16]{1,0:T(1,128)} %bitcast.31, f32[3,16]{1,0:T(4,128)} %refs_3_.3, bf16[12,768,512]{2,1,0:T(8,128)(2,1)} %bitcast.21, bf16[12,16,512]{2,1,0:T(8,128)(2,1)} %pad.4.refs_5_, s32[12,32,768]{2,1,0:T(8,128)} %bitcast.23, ...), custom_call_target="tpu_custom_call" | custom-call | flops 141557760 | bytes 7077888 | tf_op jit(solution)/shard_map/march/pallas_call | solution.py:214
  105.8 0.0 all-to-all-done.1.got_ref
  105.8 0.0 copy-start.1
  105.8 0.9 copy-done.1
  106.7 10.3 %all-to-all-start = ((s32[64,24,384]{2,1,0:T(8,128)}), s32[64,24,384]{2,1,0:T(8,128)S(1)}, u32[]{:S(2)}, u32[]{:S(2)}) async-start(s32[64,24,384]{2,1,0:T(8,128)} %march.3), calls=%async_computation | async-start | bytes 4718592 | tf_op jit(solution)/shard_map/all_to_all | solution.py:348
  117.0 3.1 %blend.2.image_ref = f32[4,12,512]{2,1,0:T(8,128)} custom-call(s32[64]{0:T(128)} %place_ref.3, s32[64,24,128]{2,1,0:T(8,128)} %copy-done.1), custom_call_target="tpu_custom_call" | custom-call | flops 7864320 | bytes 786432 | tf_op jit(solution)/shard_map/blend/pallas_call | solution.py:310
  120.0 53.9 %all-to-all-done.got_ref = s32[64,24,384]{2,1,0:T(8,128)S(1)} async-done(((s32[64,24,384]{2,1,0:T(8,128)}), s32[64,24,384]{2,1,0:T(8,128)S(1)}, u32[]{:S(2)}, u32[]{:S(2)}) %all-to-all-start) | async-done | bytes 2359328 | tf_op jit(solution)/shard_map/all_to_all | solution.py:348
  173.9 0.0 copy-start
  173.9 1.4 copy-done
  175.3 4.4 %blend.3 = f32[4,12,512]{2,1,0:T(8,128)} custom-call(s32[64]{0:T(128)} %place_ref.3, s32[64,24,384]{2,1,0:T(8,128)} %copy-done, f32[4,12,512]{2,1,0:T(8,128)} %blend.2.image_ref), custom_call_target="tpu_custom_call" | custom-call | flops 23592960 | bytes 2359296 | tf_op jit(solution)/shard_map/blend/pallas_call | solution.py:310
  179.8 1.6 copy.36
  (8 shorter events, 0.1 us)
Async XLA Ops:
  1.3 5.3 %collective-permute-start = (bf16[12,512]{1,0:T(8,128)(2,1)S(1)}, bf16[12,512]{1,0:T(8,128)(2,1)S(1)}, u32[]{:S(2)}, u32[]{:S(2)}) collective-permute-start(bf16[12,512]{1,0:T(8,128)(2,1)S(1)} %bitcast.25), channel_id=1, source_target_pairs={{0,2},{1,3},{2,0},{3,1},{4,6},{5,7},{6,4},{7,5},{8,10},{9,11},{10,... | collective-permute-start | bytes 36872 | tf_op jit(solution)/shard_map/ppermute | solution.py:24
  27.5 78.3 %all-to-all-start.1 = ((s32[64,24,128]{2,1,0:T(8,128)}), s32[64,24,128]{2,1,0:T(8,128)S(1)}, u32[]{:S(2)}, u32[]{:S(2)}) async-start(s32[64,24,128]{2,1,0:T(8,128)} %get-tuple-element.8), calls=%async_computation.1 | async-start | bytes 1572864 | tf_op jit(solution)/shard_map/all_to_all | solution.py:342
  40.7 3.9 %collective-permute-start.1 = (bf16[12,768]{1,0:T(8,128)(2,1)S(1)}, bf16[12,768]{1,0:T(8,128)(2,1)S(1)}, u32[]{:S(2)}, u32[]{:S(2)}) collective-permute-start(bf16[12,768]{1,0:T(8,128)(2,1)S(1)} %fusion.2), channel_id=1, source_target_pairs={{0,1},{1,0},{2,3},{3,2},{4,5},{5,4},{6,7},{7,6},{8,9},{9,8},{10,11... | collective-permute-start | bytes 55304 | tf_op jit(solution)/shard_map/ppermute | solution.py:24
  105.8 0.9 copy-start.1
  106.7 67.3 %all-to-all-start = ((s32[64,24,384]{2,1,0:T(8,128)}), s32[64,24,384]{2,1,0:T(8,128)S(1)}, u32[]{:S(2)}, u32[]{:S(2)}) async-start(s32[64,24,384]{2,1,0:T(8,128)} %march.3), calls=%async_computation | async-start | bytes 4718592 | tf_op jit(solution)/shard_map/all_to_all | solution.py:348
  173.9 1.4 copy-start

commit v2 on v0

v2 whole, which is shorter than its diff:
```python
import functools

import jax
import jax.numpy as jnp
from jax import lax
from jax.experimental import pallas as pl
from jax.experimental.pallas import tpu as pltpu
from jax.sharding import PartitionSpec as P

CELL = 16
LANES = 128
SIDE = 8
BAND = 256
LOG2E = 1.4426950408889634
LEVELS = 65535.0
CHUNKS = ((1, 2), (0, 3))
EDGES = 8
SHADE_GAIN = 0.7 * 0.6 * 0.6
SHADE_BASE = 0.3 / SHADE_GAIN

NT = (((1,), (1,)), ((), ()))
NN = (((1,), (0,)), ((), ()))


def from_partner(value, axis, apart):
    return lax.ppermute(value, axis, [(i, i ^ 1 << apart) for i in range(lax.axis_size(axis))])


def tile_of(tiles, j):
    tile = jnp.int32(tiles[0])
    for n in range(1, len(tiles)):
        tile = jnp.where(j == n, jnp.int32(tiles[n]), tile)
    return tile


def code(value):
    root = lax.rsqrt(lax.rsqrt(jnp.maximum(value, 0.0)))
    return jnp.minimum(root * LEVELS + 0.5, LEVELS).astype(jnp.int32)


def decode(word):
    root = word.astype(jnp.float32) * (1.0 / LEVELS)
    square = root * root
    return square * square


def march_kernel(tiles, sizes, *refs):
    steps, height, width, total = sizes
    count = len(tiles)
    center_ref, wide_ref, peak_ref, color_ref, vol_ref, rim_ref, index_ref, halo_ref = refs[:8]
    if halo_ref is None:
        out_ref, edge_ref = refs[8:10]
        scratch = refs[10:]
    else:
        out_ref = refs[8]
        edge_ref = None
        scratch = refs[9:]
    (band_ref, table_ref, left_ref, value_ref, grad_ref, param_ref, pair_a, pair_b, turn_a, turn_b) = scratch[:10]
    part = pl.program_id(0)
    halves = BAND // LANES
    groups = LANES // CELL

    @pl.when(part == 0)
    def _():
        k = lax.broadcasted_iota(jnp.int32, (BAND + LANES, BAND), 0)
        r = lax.broadcasted_iota(jnp.int32, (BAND + LANES, BAND), 1)
        rim = k >= BAND
        above = (~rim & (k == r - 1)) | (rim & (k % 2 == 0) & (r == 0))
        below = (~rim & (k == r + 1)) | (rim & (k % 2 == 1) & (r == BAND - 1))
        band_ref[...] = jnp.where(below, 1.0, jnp.where(above, -1.0, 0.0)).astype(jnp.bfloat16)
        shape = (8, 16)
        scale = (0.5 * LOG2E) ** 0.5 / wide_ref[...]
        table_ref[0, :, 0:16] = jnp.broadcast_to(center_ref[...], shape)
        table_ref[1, :, 0:16] = jnp.broadcast_to(scale, shape)
        table_ref[2, :, 0:16] = jnp.broadcast_to(jnp.log2(peak_ref[...] * (0.25 * LOG2E / total)), shape)
        for n in range(3):
            table_ref[3 + n, :, 0:16] = jnp.broadcast_to(color_ref[n : n + 1, :] * SHADE_GAIN, shape)
        if edge_ref is not None:
            spots_ref = scratch[10]
            col = lax.broadcasted_iota(jnp.int32, (width, LANES), 0)
            lane = lax.broadcasted_iota(jnp.int32, (width, LANES), 1)
            which = lane % EDGES
            want = jnp.where(which == 0, 0, (which + 1) // 2 * LANES - which % 2)
            for s in range(steps):
                hit = (col == want) & (lane // EDGES == s)
                spots_ref[s] = jnp.where(hit, 1.0, 0.0).astype(jnp.bfloat16)

    if edge_ref is not None:
        spots_ref = scratch[10]
        found = jnp.zeros((BAND, LANES), jnp.float32)
        for s in range(steps):
            found = found + lax.dot_general(vol_ref[s], spots_ref[s], NN, preferred_element_type=jnp.float32)
        edge_ref[...] = found.T

    pair_lane = lax.broadcasted_iota(jnp.int32, (LANES, LANES), 1) // 2
    rims = [rim_ref[:, LANES * t : LANES * t + LANES].astype(jnp.float32).T for t in tiles]
    batch = 3
    for q in range(steps // batch):
        for s in range(batch * q, batch * q + batch):
            for k in range(count):
                t = tiles[k]
                at = slice((s * count + k) * LANES, (s * count + k) * LANES + LANES)
                if edge_ref is None:
                    source = vol_ref[k][s]
                else:
                    source = vol_ref[s, :, LANES * t : LANES * t + LANES]
                turned = source.T
                left_ref[at, 0:BAND] = turned
                left_ref[at, BAND : BAND + LANES] = jnp.where(pair_lane == s, rims[k], 0.0).astype(jnp.bfloat16)
                for m in range(halves):
                    lanes = slice(LANES * m, LANES * m + LANES)
                    value_ref[s, k, m, SIDE : SIDE + LANES, :] = turned[:, lanes].astype(jnp.float32)
                    if edge_ref is None:
                        before = halo_ref[4 * s + 2 * k : 4 * s + 2 * k + 1, lanes]
                        after = halo_ref[4 * s + 2 * k + 1 : 4 * s + 2 * k + 2, lanes]
                    else:
                        before = edge_ref[EDGES * s + 2 * t - 1 : EDGES * s + 2 * t, lanes]
                        after = edge_ref[EDGES * s + 2 * t + 2 : EDGES * s + 2 * t + 3, lanes]
                    value_ref[s, k, m, SIDE - 1 : SIDE, :] = before
                    value_ref[s, k, m, SIDE + LANES : SIDE + LANES + 1, :] = after
                    index = index_ref[s, groups * t : groups * t + groups, lanes]
                    for p in range(6):
                        param_ref[s, p, k * halves + m] = jnp.take_along_axis(table_ref[p], index, axis=1)
        size = batch * count * LANES
        grad = lax.dot_general(left_ref[q * size : q * size + size, :], band_ref[...], NN, preferred_element_type=jnp.float32)
        for s in range(batch):
            for k in range(count):
                for m in range(halves):
                    at = (s * count + k) * LANES
                    grad_ref[q * batch + s, k * halves + m] = grad[at : at + LANES, LANES * m : LANES * m + LANES]

    def strip(i, carry):
        g = i % groups
        lane = i // groups
        k = lane // halves
        m = lane % halves
        base = pl.multiple_of(g * CELL, CELL)
        zero = jnp.zeros((8, LANES), jnp.float32)
        state = [[zero, zero + 1.0, zero, zero, zero] for _ in range(2)]
        for s in range(steps):
            param = [param_ref[s, p, lane, pl.ds(g, 8, stride=0), :] for p in range(6)]
            for u in range(2):
                depth, trans, red, green, blue = state[u]
                at = base + 8 * u
                value = value_ref[s, k, m, pl.ds(at + SIDE, 8), :]
                ahead = value_ref[s, k, m, pl.ds(at + SIDE + 1, 8), :]
                behind = value_ref[s, k, m, pl.ds(at + SIDE - 1, 8), :]
                grad_x = ahead - behind
                grad_y = grad_ref[s, lane, pl.ds(at, 8), :]
                energy = grad_x * grad_x + grad_y * grad_y
                facing = grad_x + (0.8 / 0.6) * grad_y
                shade = SHADE_BASE + facing * facing / (4.0 + energy)
                scaled = (value - param[0]) * param[1]
                rate = jnp.exp2(param[2] - scaled * scaled)
                depth = depth - rate * energy
                after = jnp.exp2(depth)
                weight = (trans - after) * shade
                red = red + weight * param[3]
                green = green + weight * param[4]
                blue = blue + weight * param[5]
                state[u] = [depth, after, red, green, blue]
        for u in range(2):
            depth, trans, red, green, blue = state[u]
            at = pl.ds(base + 8 * u, 8)
            pair_a[lane, at, :] = (code(red) << 16) | code(green)
            pair_b[lane, at, :] = (code(blue) << 16) | code(1.0 - trans)
        return carry

    lax.fori_loop(0, groups * count * halves, strip, 0)
    for k in range(count):
        for m in range(halves):
            rows = pl.ds(pl.multiple_of(part * BAND + m * LANES, LANES), LANES)
            turn_a[k, rows, :] = pair_a[k * halves + m].T
            turn_b[k, rows, :] = pair_b[k * halves + m].T

    @pl.when(part == height // BAND - 1)
    def _():
        piece = height // out_ref.shape[0]

        def pack(d, carry):
            for u in range(4):
                e = d * 4 + u
                r = e * piece
                for k in range(count):
                    lanes = slice(LANES * k, LANES * k + LANES)
                    out_ref[e, 0:8, lanes] = turn_a[k, pl.ds(r, 8), :]
                    out_ref[e, 8:12, lanes] = turn_a[k, pl.ds(r + 8, 4), :]
                    out_ref[e, 12:16, lanes] = turn_b[k, pl.ds(r + 8, 4), :]
                    out_ref[e, 16:24, lanes] = turn_b[k, pl.ds(r, 8), :]
            return carry

        lax.fori_loop(0, out_ref.shape[0] // 4, pack, 0)


def march(tiles, ranks, tables, samples, rim_rows, cells, halo):
    steps, height, width = samples.shape
    first = halo is None
    count = len(tiles)
    sizes = (steps, height, width, steps * ranks)
    halves = BAND // LANES

    def body(*refs):
        refs = list(refs)
        if first:
            refs.insert(7, None)
        else:
            refs[4 : 4 + count] = [refs[4 : 4 + count]]
        march_kernel(tiles, sizes, *refs)

    small = lambda shape: pl.BlockSpec(shape, lambda n: (0, 0))
    in_specs = [small((1, 16)), small((1, 16)), small((1, 16)), small((3, 16))]
    args = list(tables)
    if first:
        in_specs.append(pl.BlockSpec((steps, BAND, width), lambda n: (0, n, 0)))
        args.append(samples)
    else:
        for t in tiles:
            in_specs.append(pl.BlockSpec((steps, BAND, LANES), lambda n, t=t: (0, n, t)))
            args.append(samples)
    in_specs += [
        pl.BlockSpec((None, LANES, width), lambda n: (n, 0, 0)),
        pl.BlockSpec((steps, width // CELL, BAND), lambda n: (0, 0, n)),
    ]
    args += [rim_rows, cells]
    piece = height // ranks
    out_shape = [jax.ShapeDtypeStruct((ranks, 2 * piece, LANES * count), jnp.int32)]
    out_specs = [pl.BlockSpec((ranks, 2 * piece, LANES * count), lambda n: (0, 0, 0))]
    scratch = [
        pltpu.VMEM((BAND + LANES, BAND), jnp.bfloat16),
        pltpu.VMEM((6, 8, LANES), jnp.float32),
        pltpu.VMEM((steps * count * LANES, BAND + LANES), jnp.bfloat16),
        pltpu.VMEM((steps, count, halves, LANES + 2 * SIDE, LANES), jnp.float32),
        pltpu.VMEM((steps, count * halves, LANES, LANES), jnp.float32),
        pltpu.VMEM((steps, 6, count * halves, LANES // CELL, LANES), jnp.float32),
        pltpu.VMEM((count * halves, LANES, LANES), jnp.int32),
        pltpu.VMEM((count * halves, LANES, LANES), jnp.int32),
        pltpu.VMEM((count, height, LANES), jnp.int32),
        pltpu.VMEM((count, height, LANES), jnp.int32),
    ]
    if first:
        out_shape.append(jax.ShapeDtypeStruct((LANES, height), jnp.float32))
        out_specs.append(pl.BlockSpec((LANES, BAND), lambda n: (0, n)))
        scratch.append(pltpu.VMEM((steps, width, LANES), jnp.bfloat16))
    else:
        in_specs.append(pl.BlockSpec((4 * steps, BAND), lambda n: (0, n)))
        args.append(halo)
    points = steps * height * LANES * count
    return pl.pallas_call(
        body,
        grid=(height // BAND,),
        in_specs=in_specs,
        out_specs=out_specs,
        out_shape=out_shape,
        scratch_shapes=scratch,
        compiler_params=pltpu.CompilerParams(
            dimension_semantics=("arbitrary",), vmem_limit_bytes=56 * 1024 * 1024
        ),
        cost_estimate=pl.CostEstimate(flops=40 * points, bytes_accessed=2 * points, transcendentals=3 * points),
        name="march",
    )(*args)


def blend_kernel(tiles, order_ref, got_ref, out_ref):
    ranks = got_ref.shape[0]
    count = len(tiles)
    unroll = 4
    lower = lax.broadcasted_iota(jnp.int32, (8, LANES), 0) < 4
    zero = jnp.zeros((8, LANES), jnp.float32)
    one = zero + 1.0

    def layer(i, carry):
        carry = list(carry)
        for u in range(unroll):
            d = order_ref[i * unroll + u]
            for n in range(count):
                lanes = slice(LANES * n, LANES * n + LANES)
                red, green, blue, alpha, trans, high, low, half = carry[n]
                first = got_ref[d, 0:8, lanes]
                mixed = got_ref[d, 8:16, lanes]
                last = got_ref[d, 16:24, lanes]
                cover = decode(last & 0xFFFF) * trans
                red = red + trans * decode(lax.shift_right_logical(first, 16))
                green = green + trans * decode(first & 0xFFFF)
                blue = blue + trans * decode(lax.shift_right_logical(last, 16))
                alpha = alpha + cover
                trans = trans - cover
                level = decode(mixed & 0xFFFF)
                opaque = jnp.where(lower, pltpu.roll(level, 4, 0), level)
                high = high + half * decode(lax.shift_right_logical(mixed, 16))
                low = low + half * level
                half = half - half * opaque
                carry[n] = (red, green, blue, alpha, trans, high, low, half)
        return tuple(carry)

    start = tuple((zero, zero, zero, zero, one, zero, zero, one) for _ in range(count))
    final = lax.fori_loop(0, ranks // unroll, layer, start)
    for n in range(count):
        lanes = slice(LANES * tiles[n], LANES * tiles[n] + LANES)
        red, green, blue, alpha, trans, high, low, half = final[n]
        for r in range(8):
            for c, plane in enumerate((red, green, blue, alpha)):
                out_ref[c, r, :, lanes] = plane[r : r + 1]
        for r in range(4):
            for c, plane in enumerate((high, low)):
                out_ref[c, 8 + r, :, lanes] = plane[r : r + 1]
                out_ref[2 + c, 8 + r, :, lanes] = plane[4 + r : 5 + r]


def blend(tiles, order, got, image, width):
    ranks, rows, lanes = got.shape
    whole = pl.BlockSpec(memory_space=pltpu.VMEM)
    scalars = pl.BlockSpec(memory_space=pltpu.SMEM)
    picture = jax.ShapeDtypeStruct((4, rows // 2, 1, width), jnp.float32)
    cost = pl.CostEstimate(flops=40 * got.size, bytes_accessed=4 * got.size, transcendentals=0)
    got = pltpu.with_memory_space_constraint(got, pltpu.VMEM)

    def early(place_ref, got_ref, out_ref, order_ref):
        def note(d, carry):
            order_ref[place_ref[d]] = d
            return carry

        lax.fori_loop(0, ranks, note, 0)
        blend_kernel(tiles, order_ref, got_ref, out_ref)

    def late(order_ref, got_ref, image_ref, out_ref):
        out_ref[...] = image_ref[...]
        blend_kernel(tiles, order_ref, got_ref, out_ref)

    if image is None:
        return pl.pallas_call(
            early,
            in_specs=[scalars, whole],
            out_specs=[whole, scalars],
            out_shape=[picture, jax.ShapeDtypeStruct((ranks,), jnp.int32)],
            cost_estimate=cost,
            name="blend",
        )(order, got)
    return pl.pallas_call(
        late, in_specs=[scalars, whole, whole], out_specs=whole, out_shape=picture, cost_estimate=cost, name="blend"
    )(order, got, image)


def on_device(volume, table_index, brick_position, tf_center, tf_width, tf_peak, tf_color):
    samples = volume[:, 0]
    cells = jnp.swapaxes(table_index[:, 0], 1, 2)
    steps, height, width = samples.shape
    ranks = lax.axis_size("depth")
    tables = [tf_center[None], tf_width[None], tf_peak[None], tf_color]
    tile_rank = lax.axis_index("tile")
    col_bit = tile_rank % 2
    row_bit = tile_rank // 2
    send_row = jnp.where(row_bit == 0, samples[:, height - 1, :], samples[:, 0, :])
    got_row = from_partner(send_row, "tile", 1)
    zero_row = jnp.zeros_like(got_row)
    ends = [jnp.where(row_bit == 1, got_row, zero_row)]
    for n in range(1, height // BAND):
        ends += [samples[:, BAND * n, :], samples[:, BAND * n - 1, :]]
    ends += [jnp.where(row_bit == 0, got_row, zero_row)]
    bands = height // BAND
    rim_rows = jnp.stack([jnp.stack(ends[2 * n : 2 * n + 2], axis=1) for n in range(bands)], axis=0)
    rim_rows = rim_rows.reshape(bands, 2 * steps, width)
    rim_rows = jnp.pad(rim_rows, ((0, 0), (0, LANES - 2 * steps), (0, 0)))
    early, edges = march(CHUNKS[0], ranks, tables, samples, rim_rows, cells, None)
    swap = functools.partial(lax.all_to_all, axis_name="depth", split_axis=0, concat_axis=0, tiled=True)
    got_early = swap(early)
    edges = edges[: EDGES * steps].reshape(steps, EDGES, height)
    send_col = jnp.where(col_bit == 0, edges[:, 7], edges[:, 0]).astype(jnp.bfloat16)
    got_col = from_partner(send_col, "tile", 0).astype(jnp.float32)
    zero_col = jnp.zeros_like(got_col)
    lines = [jnp.where(col_bit == 1, got_col, zero_col), edges[:, 2], edges[:, 5], jnp.where(col_bit == 0, got_col, zero_col)]
    halo = jnp.stack(lines, axis=1).reshape(4 * steps, height)
    (late,) = march(CHUNKS[1], ranks, tables, samples, rim_rows, cells, halo)
    got_late = swap(late)
    image, order = blend(CHUNKS[0], brick_position, got_early, None, width)
    image = blend(CHUNKS[1], order, got_late, image, width)
    return jnp.swapaxes(image, 1, 2)


def solution(mesh):
    return jax.shard_map(
        on_device,
        mesh=mesh,
        in_specs=(
            P("depth", "tile", None, None),
            P("depth", "tile", None, None),
            P(),
            P(),
            P(),
            P(),
            P(),
        ),
        out_specs=P(None, "tile", "depth", None),
        check_vma=False,
    )
```

time: 435 us -> 132 us (0.30)
  other arithmetic: 139 us -> 2.38 us
  local copies, waits for them, and re-layouts: 133 us -> 1.01 us
  waiting for transfers between devices: 143 us -> 57.2 us
  Pallas kernels: 0 us -> 49.5 us
  starting transfers between devices: 15.2 us -> 21.2 us
    all_to_all x1 -> x2, waiting for transfers between devices: 141 us -> 51.7 us  [the longest x1 37.2 us: on_device(): got_late = swap(late)]
    pallas_call x0 -> x4, Pallas kernels: none -> 49.5 us  [the longest x2 44 us: march(): pl.pallas_call(body, grid=(height // BAND,), in_specs=in_specs, out_specs...]
    slice x34 -> x2, local copies, waits for them, and re-layouts: 41.2 us -> 0.11 us  [the longest x1 0.06 us: on_device(): edges[:, 2]]
    while x86 -> x0, local copies, waits for them, and re-layouts: 36.1 us -> none
    convert_element_type x24 -> x1, other arithmetic: 30.8 us -> 0.01 us  [on_device(): jnp.where(col_bit == 0, edges[:, 7], edges[:, 0]).astype(jnp.bfloat16)]
    add x18 -> x0, other arithmetic: 29.6 us -> none  [the longest x12 21.8 us: light_sample(): rgb = rgb + weight[None] * params[3:6] * shade[None]]
    mul x29 -> x0, other arithmetic: 27.4 us -> none  [the longest x12 22.4 us: light_sample(): trans = trans * keep]
    unnamed x22 -> x3, local copies, waits for them, and re-layouts: 27.4 us -> 0.01 us
  transfers between devices with their start and end apart: 3 -> 4, of which waited for: 2 -> 4; matrix products, arithmetic and copies ran while one was open for 6% -> 1% of each run, Pallas kernels for 0% -> 18%
where the time goes in v2:
time: 132 us; the launch traced here: 131 us
  waiting for transfers between devices  57.2 us (43%)
  Pallas kernels  49.5 us (38%)
  starting transfers between devices  21.2 us (16%)
  other arithmetic  2.38 us (2%)
    pallas_call x2, Pallas kernels, march(): pl.pallas_call(body, grid=(height // BAND,), in_specs=in_specs, out_specs...  44 us
    all_to_all x1, waiting for transfers between devices, on_device(): got_late = swap(late)  37.2 us
    all_to_all x1, waiting for transfers between devices, on_device(): got_early = swap(early)  14.5 us
    all_to_all x1, starting transfers between devices, on_device(): got_early = swap(early)  12.2 us
    ppermute x2, waiting for transfers between devices, from_partner(): lax.ppermute(value, axis, [(i, i ^ 1 << apart) for i in range(lax.axis_si...  5.5 us
    all_to_all x1, starting transfers between devices, on_device(): got_late = swap(late)  5.34 us
    ppermute x2, starting transfers between devices, from_partner(): lax.ppermute(value, axis, [(i, i ^ 1 << apart) for i in range(lax.axis_si...  3.58 us
    pallas_call x1, Pallas kernels, blend(): pl.pallas_call(early, in_specs=[scalars, whole], out_specs=[whole, scalar...  2.9 us
  transfers between devices with their start and end apart: 4, of which 4 were waited for; matrix products, arithmetic and copies ran while one was open for 1% of the time, Pallas kernels for 18%

profile of v2, /device:TPU:4, one launch (start us, length us, event | category | flops | bytes accessed | tf_op | source)
XLA Modules:
  0.0 131.4 jit_solution(3638125600940431932)
XLA Ops:
  0.0 1.3 fusion.8
  1.3 2.3 %collective-permute-start = (bf16[12,512]{1,0:T(8,128)(2,1)S(1)}, bf16[12,512]{1,0:T(8,128)(2,1)S(1)}, u32[]{:S(2)}, u32[]{:S(2)}) collective-permute-start(bf16[12,512]{1,0:T(8,128)(2,1)S(1)} %bitcast.27), channel_id=1, source_target_pairs={{0,2},{1,3},{2,0},{3,1},{4,6},{5,7},{6,4},{7,5},{8,10},{9,11},{10,... | collective-permute-start | bytes 36872 | tf_op jit(solution)/shard_map/ppermute | solution.py:26
  3.6 0.1 pad_maximum_fusion.2
  3.7 2.9 %collective-permute-done = bf16[12,512]{1,0:T(8,128)(2,1)S(1)} collective-permute-done((bf16[12,512]{1,0:T(8,128)(2,1)S(1)}, bf16[12,512]{1,0:T(8,128)(2,1)S(1)}, u32[]{:S(2)}, u32[]{:S(2)}) %collective-permute-start) | collective-permute-done | bytes 12320 | tf_op jit(solution)/shard_map/ppermute | solution.py:26
  6.7 0.1 pad_maximum_fusion.1
  6.8 0.8 fusion.4.refs_5_.refs_6_
  7.6 23.5 %march.2 = (s32[64,24,256]{2,1,0:T(8,128)}, f32[128,768]{1,0:T(8,128)}) custom-call(f32[1,16]{1,0:T(1,128)} %bitcast.28, f32[1,16]{1,0:T(1,128)} %bitcast.30, f32[1,16]{1,0:T(1,128)} %bitcast.32, f32[3,16]{1,0:T(4,128)} %refs_3_.3, bf16[12,768,512]{2,1,0:T(8,128)(2,1)} %bitcast.22, bf16[3,128,512]{2,1,0:T(8,128)(2,1)} %fusion.4.refs_5_.refs_6_, ...), custom_call_target="tpu_custom_call" | custom-call | flops 94371840 | bytes 4718592 | tf_op jit(solution)/shard_map/march/pallas_call | solution.py:248
  31.1 0.0 copy-start
  31.1 12.2 %all-to-all-start = ((s32[64,24,256]{2,1,0:T(8,128)}), s32[64,24,256]{2,1,0:T(8,128)S(1)}, u32[]{:S(2)}, u32[]{:S(2)}) async-start(s32[64,24,256]{2,1,0:T(8,128)} %get-tuple-element.9), calls=%async_computation | async-start | bytes 3145728 | tf_op jit(solution)/shard_map/all_to_all | solution.py:365
  43.3 0.0 copy-done
  43.4 1.3 collective-permute-start.1
  44.7 0.1 fusion.9
  44.8 2.6 %collective-permute-done.1 = bf16[12,768]{1,0:T(8,128)(2,1)S(1)} collective-permute-done((bf16[12,768]{1,0:T(8,128)(2,1)S(1)}, bf16[12,768]{1,0:T(8,128)(2,1)S(1)}, u32[]{:S(2)}, u32[]{:S(2)}) %collective-permute-start.1) | collective-permute-done | bytes 18464 | tf_op jit(solution)/shard_map/ppermute | solution.py:26
  47.5 0.1 pad_maximum_fusion
  47.6 0.7 reshape.19.refs_8_
  48.3 20.6 %march.3 = s32[64,24,256]{2,1,0:T(8,128)} custom-call(f32[1,16]{1,0:T(1,128)} %bitcast.29, f32[1,16]{1,0:T(1,128)} %bitcast.31, f32[1,16]{1,0:T(1,128)} %bitcast.33, f32[3,16]{1,0:T(4,128)} %refs_3_.3, bf16[12,768,512]{2,1,0:T(8,128)(2,1)} %bitcast.23, bf16[12,768,512]{2,1,0:T(8,128)(2,1)} %bitcast.24, bf16[3,128,512]{2,1,0:T(8,128)(2,1)} %fusion.4.refs_5_.refs_6_, ...), custom_call_target="tpu_custom_call" | custom-call | flops 94371840 | bytes 4718592 | tf_op jit(solution)/shard_map/march/pallas_call | solution.py:248
  68.9 14.5 %all-to-all-done.got_ref = s32[64,24,256]{2,1,0:T(8,128)S(1)} async-done(((s32[64,24,256]{2,1,0:T(8,128)}), s32[64,24,256]{2,1,0:T(8,128)S(1)}, u32[]{:S(2)}, u32[]{:S(2)}) %all-to-all-start) | async-done | bytes 1572896 | tf_op jit(solution)/shard_map/all_to_all | solution.py:365
  83.4 5.3 %all-to-all-start.1 = ((s32[64,24,256]{2,1,0:T(8,128)}), s32[64,24,256]{2,1,0:T(8,128)S(1)}, u32[]{:S(2)}, u32[]{:S(2)}) async-start(s32[64,24,256]{2,1,0:T(8,128)} %march.3), calls=%async_computation.1 | async-start | bytes 3145728 | tf_op jit(solution)/shard_map/all_to_all | solution.py:373
  88.8 2.9 %blend.2 = (f32[4,12,1,512]{3,2,1,0:T(1,128)}, s32[64]{0:T(128)}) custom-call(s32[64]{0:T(128)} %place_ref.1, s32[64,24,256]{2,1,0:T(8,128)S(1)} %all-to-all-done.got_ref), custom_call_target="tpu_custom_call" | custom-call | flops 15728640 | bytes 1572864 | tf_op jit(solution)/shard_map/blend/pallas_call | solution.py:330
  91.7 37.2 %all-to-all-done.1.got_ref = s32[64,24,256]{2,1,0:T(8,128)S(1)} async-done(((s32[64,24,256]{2,1,0:T(8,128)}), s32[64,24,256]{2,1,0:T(8,128)S(1)}, u32[]{:S(2)}, u32[]{:S(2)}) %all-to-all-start.1) | async-done | bytes 1572896 | tf_op jit(solution)/shard_map/all_to_all | solution.py:373
  128.9 2.5 %blend.3 = f32[4,12,1,512]{3,2,1,0:T(1,128)} custom-call(s32[64]{0:T(128)} %get-tuple-element.10.order_ref, s32[64,24,256]{2,1,0:T(8,128)S(1)} %all-to-all-done.1.got_ref, f32[4,12,1,512]{3,2,1,0:T(1,128)} %get-tuple-element.12.image_ref), custom_call_target="tpu_custom_call" | custom-call | flops 15728640 | bytes 1572864 | tf_op jit(solution)/shard_map/blend/pallas_call | solution.py:338
  (13 shorter events, 0.3 us)
Async XLA Ops:
  1.3 5.3 %collective-permute-start = (bf16[12,512]{1,0:T(8,128)(2,1)S(1)}, bf16[12,512]{1,0:T(8,128)(2,1)S(1)}, u32[]{:S(2)}, u32[]{:S(2)}) collective-permute-start(bf16[12,512]{1,0:T(8,128)(2,1)S(1)} %bitcast.27), channel_id=1, source_target_pairs={{0,2},{1,3},{2,0},{3,1},{4,6},{5,7},{6,4},{7,5},{8,10},{9,11},{10,... | collective-permute-start | bytes 36872 | tf_op jit(solution)/shard_map/ppermute | solution.py:26
  31.1 12.3 %copy-start = (f32[128,768]{1,0:T(8,128)S(1)}, f32[128,768]{1,0:T(8,128)}, u32[]{:S(2)}) copy-start(f32[128,768]{1,0:T(8,128)} %get-tuple-element.11) | copy-start | bytes 1179652
  31.1 52.3 %all-to-all-start = ((s32[64,24,256]{2,1,0:T(8,128)}), s32[64,24,256]{2,1,0:T(8,128)S(1)}, u32[]{:S(2)}, u32[]{:S(2)}) async-start(s32[64,24,256]{2,1,0:T(8,128)} %get-tuple-element.9), calls=%async_computation | async-start | bytes 3145728 | tf_op jit(solution)/shard_map/all_to_all | solution.py:365
  43.4 3.9 %collective-permute-start.1 = (bf16[12,768]{1,0:T(8,128)(2,1)S(1)}, bf16[12,768]{1,0:T(8,128)(2,1)S(1)}, u32[]{:S(2)}, u32[]{:S(2)}) collective-permute-start(bf16[12,768]{1,0:T(8,128)(2,1)S(1)} %fusion.7), channel_id=1, source_target_pairs={{0,1},{1,0},{2,3},{3,2},{4,5},{5,4},{6,7},{7,6},{8,9},{9,8},{10,11... | collective-permute-start | bytes 55304 | tf_op jit(solution)/shard_map/ppermute | solution.py:26
  83.4 45.4 %all-to-all-start.1 = ((s32[64,24,256]{2,1,0:T(8,128)}), s32[64,24,256]{2,1,0:T(8,128)S(1)}, u32[]{:S(2)}, u32[]{:S(2)}) async-start(s32[64,24,256]{2,1,0:T(8,128)} %march.3), calls=%async_computation.1 | async-start | bytes 3145728 | tf_op jit(solution)/shard_map/all_to_all | solution.py:373

commit v3 on v2

--- a/solution.py
+++ b/solution.py
@@ -7,18 +7,20 @@
 from jax.experimental.pallas import tpu as pltpu
 from jax.sharding import PartitionSpec as P
 
+
 CELL = 16
 LANES = 128
 SIDE = 8
 BAND = 256
 LOG2E = 1.4426950408889634
 LEVELS = 65535.0
+SCALE = LEVELS**4
 CHUNKS = ((1, 2), (0, 3))
 EDGES = 8
+STRIP = 4
 SHADE_GAIN = 0.7 * 0.6 * 0.6
 SHADE_BASE = 0.3 / SHADE_GAIN
 
-NT = (((1,), (1,)), ((), ()))
 NN = (((1,), (0,)), ((), ()))
 
 
@@ -26,16 +28,9 @@
     return lax.ppermute(value, axis, [(i, i ^ 1 << apart) for i in range(lax.axis_size(axis))])
 
 
-def tile_of(tiles, j):
-    tile = jnp.int32(tiles[0])
-    for n in range(1, len(tiles)):
-        tile = jnp.where(j == n, jnp.int32(tiles[n]), tile)
-    return tile
-
-
 def code(value):
     root = lax.rsqrt(lax.rsqrt(jnp.maximum(value, 0.0)))
-    return jnp.minimum(root * LEVELS + 0.5, LEVELS).astype(jnp.int32)
+    return jnp.minimum(root + 0.5, LEVELS).astype(jnp.int32)
 
 
 def decode(word):
@@ -44,17 +39,14 @@
     return square * square
 
 
-def march_kernel(tiles, sizes, *refs):
+def march_kernel(tiles, spans, sizes, *refs):
     steps, height, width, total = sizes
+    middle = len(spans) == 1
     count = len(tiles)
-    center_ref, wide_ref, peak_ref, color_ref, vol_ref, rim_ref, index_ref, halo_ref = refs[:8]
-    if halo_ref is None:
-        out_ref, edge_ref = refs[8:10]
-        scratch = refs[10:]
-    else:
-        out_ref = refs[8]
-        edge_ref = None
-        scratch = refs[9:]
+    center_ref, wide_ref, peak_ref, color_ref, vol_ref, rim_ref, index_ref, outer_ref, edge_ref = refs[:9]
+    first = outer_ref is None
+    out_ref, done_a, done_b = refs[9:12]
+    scratch = refs[12:]
     (band_ref, table_ref, left_ref, value_ref, grad_ref, param_ref, pair_a, pair_b, turn_a, turn_b) = scratch[:10]
     part = pl.program_id(0)
     halves = BAND // LANES
@@ -74,33 +66,35 @@
         table_ref[1, :, 0:16] = jnp.broadcast_to(scale, shape)
         table_ref[2, :, 0:16] = jnp.broadcast_to(jnp.log2(peak_ref[...] * (0.25 * LOG2E / total)), shape)
         for n in range(3):
-            table_ref[3 + n, :, 0:16] = jnp.broadcast_to(color_ref[n : n + 1, :] * SHADE_GAIN, shape)
-        if edge_ref is not None:
+            table_ref[3 + n, :, 0:16] = jnp.broadcast_to(color_ref[n : n + 1, :] * (SHADE_GAIN * SCALE), shape)
+        if first:
             spots_ref = scratch[10]
             col = lax.broadcasted_iota(jnp.int32, (width, LANES), 0)
             lane = lax.broadcasted_iota(jnp.int32, (width, LANES), 1)
             which = lane % EDGES
             want = jnp.where(which == 0, 0, (which + 1) // 2 * LANES - which % 2)
-            for s in range(steps):
-                hit = (col == want) & (lane // EDGES == s)
-                spots_ref[s] = jnp.where(hit, 1.0, 0.0).astype(jnp.bfloat16)
-
-    if edge_ref is not None:
+            spots_ref[...] = jnp.where(col == want, 1.0, 0.0).astype(jnp.bfloat16)
+
+    if first:
         spots_ref = scratch[10]
+        rows = vol_ref[...].reshape(steps * BAND, width)
+        seen = lax.dot_general(rows, spots_ref[...], NN, preferred_element_type=jnp.float32)
+        owner = lax.broadcasted_iota(jnp.int32, (BAND, LANES), 1) // EDGES
         found = jnp.zeros((BAND, LANES), jnp.float32)
         for s in range(steps):
-            found = found + lax.dot_general(vol_ref[s], spots_ref[s], NN, preferred_element_type=jnp.float32)
-        edge_ref[...] = found.T
+            found = jnp.where(owner == s, seen[BAND * s : BAND * s + BAND], found)
+        for m in range(halves):
+            edge_ref[m] = found[LANES * m : LANES * m + LANES].T
 
     pair_lane = lax.broadcasted_iota(jnp.int32, (LANES, LANES), 1) // 2
     rims = [rim_ref[:, LANES * t : LANES * t + LANES].astype(jnp.float32).T for t in tiles]
-    batch = 3
+    batch = 6
     for q in range(steps // batch):
         for s in range(batch * q, batch * q + batch):
             for k in range(count):
                 t = tiles[k]
                 at = slice((s * count + k) * LANES, (s * count + k) * LANES + LANES)
-                if edge_ref is None:
+                if not first:
                     source = vol_ref[k][s]
                 else:
                     source = vol_ref[s, :, LANES * t : LANES * t + LANES]
@@ -110,12 +104,14 @@
                 for m in range(halves):
                     lanes = slice(LANES * m, LANES * m + LANES)
                     value_ref[s, k, m, SIDE : SIDE + LANES, :] = turned[:, lanes].astype(jnp.float32)
-                    if edge_ref is None:
-                        before = halo_ref[4 * s + 2 * k : 4 * s + 2 * k + 1, lanes]
-                        after = halo_ref[4 * s + 2 * k + 1 : 4 * s + 2 * k + 2, lanes]
+                    if t == 0:
+                        before = outer_ref[0, s : s + 1, lanes]
                     else:
-                        before = edge_ref[EDGES * s + 2 * t - 1 : EDGES * s + 2 * t, lanes]
-                        after = edge_ref[EDGES * s + 2 * t + 2 : EDGES * s + 2 * t + 3, lanes]
+                        before = edge_ref[m, EDGES * s + 2 * t - 1 : EDGES * s + 2 * t, :]
+                    if t == width // LANES - 1:
+                        after = outer_ref[1, s : s + 1, lanes]
+                    else:
+                        after = edge_ref[m, EDGES * s + 2 * t + 2 : EDGES * s + 2 * t + 3, :]
                     value_ref[s, k, m, SIDE - 1 : SIDE, :] = before
                     value_ref[s, k, m, SIDE + LANES : SIDE + LANES + 1, :] = after
                     index = index_ref[s, groups * t : groups * t + groups, lanes]
@@ -130,16 +126,17 @@
                     grad_ref[q * batch + s, k * halves + m] = grad[at : at + LANES, LANES * m : LANES * m + LANES]
 
     def strip(i, carry):
-        g = i % groups
-        lane = i // groups
+        g = i % (groups // STRIP) * STRIP
+        lane = i // (groups // STRIP)
         k = lane // halves
         m = lane % halves
         base = pl.multiple_of(g * CELL, CELL)
         zero = jnp.zeros((8, LANES), jnp.float32)
-        state = [[zero, zero + 1.0, zero, zero, zero] for _ in range(2)]
+        state = [[zero, zero + 1.0, zero, zero, zero] for _ in range(2 * STRIP)]
         for s in range(steps):
-            param = [param_ref[s, p, lane, pl.ds(g, 8, stride=0), :] for p in range(6)]
-            for u in range(2):
+            for u in range(2 * STRIP):
+                if u % 2 == 0:
+                    param = [param_ref[s, p, lane, pl.ds(g + u // 2, 8, stride=0), :] for p in range(6)]
                 depth, trans, red, green, blue = state[u]
                 at = base + 8 * u
                 value = value_ref[s, k, m, pl.ds(at + SIDE, 8), :]
@@ -159,22 +156,33 @@
                 green = green + weight * param[4]
                 blue = blue + weight * param[5]
                 state[u] = [depth, after, red, green, blue]
-        for u in range(2):
+        for u in range(2 * STRIP):
             depth, trans, red, green, blue = state[u]
             at = pl.ds(base + 8 * u, 8)
             pair_a[lane, at, :] = (code(red) << 16) | code(green)
-            pair_b[lane, at, :] = (code(blue) << 16) | code(1.0 - trans)
+            pair_b[lane, at, :] = (code(blue) << 16) | code((1.0 - trans) * SCALE)
         return carry
 
-    lax.fori_loop(0, groups * count * halves, strip, 0)
+    lax.fori_loop(0, groups // STRIP * count * halves, strip, 0)
     for k in range(count):
         for m in range(halves):
-            rows = pl.ds(pl.multiple_of(part * BAND + m * LANES, LANES), LANES)
-            turn_a[k, rows, :] = pair_a[k * halves + m].T
-            turn_b[k, rows, :] = pair_b[k * halves + m].T
-
-    @pl.when(part == height // BAND - 1)
+            if middle:
+                rows = slice(m * LANES, m * LANES + LANES)
+                done_a[k, rows, :] = pair_a[k * halves + m].T
+                done_b[k, rows, :] = pair_b[k * halves + m].T
+            else:
+                row = part * (BAND * (spans[1] - spans[0])) + (BAND * spans[0] + m * LANES)
+                rows = pl.ds(pl.multiple_of(row, LANES), LANES)
+                turn_a[k, rows, :] = pair_a[k * halves + m].T
+                turn_b[k, rows, :] = pair_b[k * halves + m].T
+    if middle:
+        return
+
+    @pl.when(part == len(spans) - 1)
     def _():
+        if done_a is not None:
+            turn_a[:, BAND : 2 * BAND, :] = done_a[...]
+            turn_b[:, BAND : 2 * BAND, :] = done_b[...]
         piece = height // out_ref.shape[0]
 
         def pack(d, carry):
@@ -192,39 +200,50 @@
         lax.fori_loop(0, out_ref.shape[0] // 4, pack, 0)
 
 
-def march(tiles, ranks, tables, samples, rim_rows, cells, halo):
+def march(tiles, spans, ranks, tables, samples, rim_rows, cells, outer=None, edges=None, done=None):
     steps, height, width = samples.shape
-    first = halo is None
+    first = outer is None
+    middle = len(spans) == 1
     count = len(tiles)
-    sizes = (steps, height, width, steps * ranks)
     halves = BAND // LANES
+    at = lambda n: spans[0] + n * (spans[-1] - spans[0]) // max(len(spans) - 1, 1)
 
     def body(*refs):
         refs = list(refs)
-        if first:
-            refs.insert(7, None)
+        if not first:
+            refs[4 : 4 + count] = [refs[4 : 4 + count]]
+            refs[10:10] = [None, None]
+        elif middle:
+            done_a, done_b, edge = refs[7:10]
+            refs[7:10] = [None, edge, None, done_a, done_b]
         else:
-            refs[4 : 4 + count] = [refs[4 : 4 + count]]
-        march_kernel(tiles, sizes, *refs)
-
-    small = lambda shape: pl.BlockSpec(shape, lambda n: (0, 0))
+            done_a, done_b, out, edge = refs[7:11]
+            refs[7:11] = [None, edge, out, done_a, done_b]
+        march_kernel(tiles, spans, (steps, height, width, steps * ranks), *refs)
+
+    small = lambda shape: pl.BlockSpec(shape, lambda n: (0,) * len(shape))
     in_specs = [small((1, 16)), small((1, 16)), small((1, 16)), small((3, 16))]
     args = list(tables)
     if first:
-        in_specs.append(pl.BlockSpec((steps, BAND, width), lambda n: (0, n, 0)))
+        in_specs.append(pl.BlockSpec((steps, BAND, width), lambda n: (0, at(n), 0)))
         args.append(samples)
     else:
         for t in tiles:
-            in_specs.append(pl.BlockSpec((steps, BAND, LANES), lambda n, t=t: (0, n, t)))
+            in_specs.append(pl.BlockSpec((steps, BAND, LANES), lambda n, t=t: (0, at(n), t)))
             args.append(samples)
     in_specs += [
         pl.BlockSpec((None, LANES, width), lambda n: (n, 0, 0)),
-        pl.BlockSpec((steps, width // CELL, BAND), lambda n: (0, 0, n)),
+        pl.BlockSpec((steps, width // CELL, BAND), lambda n: (0, 0, at(n))),
     ]
     args += [rim_rows, cells]
-    piece = height // ranks
-    out_shape = [jax.ShapeDtypeStruct((ranks, 2 * piece, LANES * count), jnp.int32)]
-    out_specs = [pl.BlockSpec((ranks, 2 * piece, LANES * count), lambda n: (0, 0, 0))]
+    shape = (ranks, 2 * height // ranks, LANES * count)
+    half = (count, BAND, LANES)
+    if middle:
+        out_shape = [jax.ShapeDtypeStruct(half, jnp.int32)] * 2
+        out_specs = [small(half)] * 2
+    else:
+        out_shape = [jax.ShapeDtypeStruct(shape, jnp.int32)]
+        out_specs = [small(shape)]
     scratch = [
         pltpu.VMEM((BAND + LANES, BAND), jnp.bfloat16),
         pltpu.VMEM((6, 8, LANES), jnp.float32),
@@ -238,16 +257,20 @@
         pltpu.VMEM((count, height, LANES), jnp.int32),
     ]
     if first:
-        out_shape.append(jax.ShapeDtypeStruct((LANES, height), jnp.float32))
-        out_specs.append(pl.BlockSpec((LANES, BAND), lambda n: (0, n)))
-        scratch.append(pltpu.VMEM((steps, width, LANES), jnp.bfloat16))
+        out_shape.append(jax.ShapeDtypeStruct((len(spans) * halves, LANES, LANES), jnp.float32))
+        out_specs.append(pl.BlockSpec((halves, LANES, LANES), lambda n: (n, 0, 0)))
+        scratch.append(pltpu.VMEM((width, LANES), jnp.bfloat16))
+        if done is not None:
+            in_specs += [small(half)] * 2
+            args += done
     else:
-        in_specs.append(pl.BlockSpec((4 * steps, BAND), lambda n: (0, n)))
-        args.append(halo)
-    points = steps * height * LANES * count
+        in_specs.append(pl.BlockSpec((2, 16, BAND), lambda n: (0, 0, n)))
+        in_specs.append(pl.BlockSpec((halves, LANES, LANES), lambda n: (n, 0, 0)))
+        args += [outer, edges]
+    points = steps * BAND * len(spans) * LANES * count
     return pl.pallas_call(
         body,
-        grid=(height // BAND,),
+        grid=(len(spans),),
         in_specs=in_specs,
         out_specs=out_specs,
         out_shape=out_shape,
@@ -296,7 +319,7 @@
     final = lax.fori_loop(0, ranks // unroll, layer, start)
     for n in range(count):
         lanes = slice(LANES * tiles[n], LANES * tiles[n] + LANES)
-        red, green, blue, alpha, trans, high, low, half = final[n]
+        red, green, blue, alpha, _, high, low, _ = final[n]
         for r in range(8):
             for c, plane in enumerate((red, green, blue, alpha)):
                 out_ref[c, r, :, lanes] = plane[r : r + 1]
@@ -307,7 +330,7 @@
 
 
 def blend(tiles, order, got, image, width):
-    ranks, rows, lanes = got.shape
+    ranks, rows, _ = got.shape
     whole = pl.BlockSpec(memory_space=pltpu.VMEM)
     scalars = pl.BlockSpec(memory_space=pltpu.SMEM)
     picture = jax.ShapeDtypeStruct((4, rows // 2, 1, width), jnp.float32)
@@ -349,27 +372,30 @@
     tile_rank = lax.axis_index("tile")
     col_bit = tile_rank % 2
     row_bit = tile_rank // 2
+    bands = height // BAND
+    bare = [samples[:, n, :] for n in range(height) if 0 < n and n % BAND in (0, BAND - 1) and n < height - 1]
+    pad = ((0, 0), (0, LANES - 2 * steps), (0, 0))
     send_row = jnp.where(row_bit == 0, samples[:, height - 1, :], samples[:, 0, :])
+    inner_rows = jnp.pad(jnp.stack(bare[0:1] + bare[3:4], axis=1).reshape(1, 2 * steps, width), pad)
     got_row = from_partner(send_row, "tile", 1)
+    *done, middle = march(CHUNKS[0], (1,), ranks, tables, samples, inner_rows, cells)
     zero_row = jnp.zeros_like(got_row)
-    ends = [jnp.where(row_bit == 1, got_row, zero_row)]
-    for n in range(1, height // BAND):
-        ends += [samples[:, BAND * n, :], samples[:, BAND * n - 1, :]]
-    ends += [jnp.where(row_bit == 0, got_row, zero_row)]
-    bands = height // BAND
-    rim_rows = jnp.stack([jnp.stack(ends[2 * n : 2 * n + 2], axis=1) for n in range(bands)], axis=0)
-    rim_rows = rim_rows.reshape(bands, 2 * steps, width)
-    rim_rows = jnp.pad(rim_rows, ((0, 0), (0, LANES - 2 * steps), (0, 0)))
-    early, edges = march(CHUNKS[0], ranks, tables, samples, rim_rows, cells, None)
+    above = [jnp.where(row_bit == 1, got_row, zero_row), bare[1]]
+    below = [bare[2], jnp.where(row_bit == 0, got_row, zero_row)]
+    outer_rows = jnp.stack([jnp.stack(above, axis=1), jnp.stack(below, axis=1)], axis=0)
+    outer_rows = jnp.pad(outer_rows.reshape(2, 2 * steps, width), pad)
+    early, ends = march(CHUNKS[0], (0, bands - 1), ranks, tables, samples, outer_rows, cells, done=done)
     swap = functools.partial(lax.all_to_all, axis_name="depth", split_axis=0, concat_axis=0, tiled=True)
     got_early = swap(early)
-    edges = edges[: EDGES * steps].reshape(steps, EDGES, height)
-    send_col = jnp.where(col_bit == 0, edges[:, 7], edges[:, 0]).astype(jnp.bfloat16)
-    got_col = from_partner(send_col, "tile", 0).astype(jnp.float32)
-    zero_col = jnp.zeros_like(got_col)
-    lines = [jnp.where(col_bit == 1, got_col, zero_col), edges[:, 2], edges[:, 5], jnp.where(col_bit == 0, got_col, zero_col)]
-    halo = jnp.stack(lines, axis=1).reshape(4 * steps, height)
-    (late,) = march(CHUNKS[1], ranks, tables, samples, rim_rows, cells, halo)
+    halves = BAND // LANES
+    edges = jnp.concatenate([ends[:halves], middle, ends[halves:]], axis=0)
+    marks = edges[:, : EDGES * steps].reshape(height // LANES, steps, EDGES, LANES)
+    marks = jnp.where(col_bit == 0, marks[:, :, EDGES - 1], marks[:, :, 0])
+    send_col = jnp.swapaxes(marks, 0, 1).reshape(steps, height).astype(jnp.bfloat16)
+    got_col = jnp.pad(from_partner(send_col, "tile", 0).astype(jnp.float32), ((0, 16 - steps), (0, 0)))
+    outer = jnp.stack([jnp.where(col_bit == 1, got_col, 0.0), jnp.where(col_bit == 0, got_col, 0.0)], axis=0)
+    rows = jnp.concatenate([outer_rows[:1], inner_rows, outer_rows[1:]], axis=0)
+    (late,) = march(CHUNKS[1], tuple(range(bands)), ranks, tables, samples, rows, cells, outer, edges)
     got_late = swap(late)
     image, order = blend(CHUNKS[0], brick_position, got_early, None, width)
     image = blend(CHUNKS[1], order, got_late, image, width)

time: 132 us -> 131 us (level)
  the two profiles are of different devices: /device:TPU:4 before, /device:TPU:1 now
where the time goes in v3:
time: 131 us; the launch traced here: 130 us
  waiting for transfers between devices  54.9 us (42%)
  Pallas kernels  47.1 us (36%)
  starting transfers between devices  23.2 us (18%)
  other arithmetic  3.64 us (3%)
    pallas_call x3, Pallas kernels, march(): pl.pallas_call(body, grid=(len(spans),), in_specs=in_specs, out_specs=out...  41.6 us
    all_to_all x1, waiting for transfers between devices, on_device(): got_late = swap(late)  36.1 us
    all_to_all x1, waiting for transfers between devices, on_device(): got_early = swap(early)  17.2 us
    all_to_all x1, starting transfers between devices, on_device(): got_early = swap(early)  12.7 us
    all_to_all x1, starting transfers between devices, on_device(): got_late = swap(late)  6.38 us
    ppermute x2, starting transfers between devices, from_partner(): lax.ppermute(value, axis, [(i, i ^ 1 << apart) for i in range(lax.axis_si...  4.05 us
    pallas_call x1, Pallas kernels, blend(): pl.pallas_call(early, in_specs=[scalars, whole], out_specs=[whole, scalar...  2.91 us
  transfers between devices with their start and end apart: 4, of which 3 were waited for; matrix products, arithmetic and copies ran while one was open for 2% of the time, Pallas kernels for 23%

profile of v3, /device:TPU:1, one launch (start us, length us, event | category | flops | bytes accessed | tf_op | source)
XLA Modules:
  0.0 130.2 jit_solution(3584569885473630850)
XLA Ops:
  0.0 1.3 fusion.7
  1.3 3.6 %collective-permute-start = (bf16[12,512]{1,0:T(8,128)(2,1)S(1)}, bf16[12,512]{1,0:T(8,128)(2,1)S(1)}, u32[]{:S(2)}, u32[]{:S(2)}) collective-permute-start(bf16[12,512]{1,0:T(8,128)(2,1)S(1)} %bitcast.38), channel_id=1, source_target_pairs={{0,2},{1,3},{2,0},{3,1},{4,6},{5,7},{6,4},{7,5},{8,10},{9,11},{10,... | collective-permute-start | bytes 36872 | tf_op jit(solution)/shard_map/ppermute | solution.py:28
  4.9 0.1 pad_maximum_fusion.5
  5.0 0.7 pad.16.refs_5_
  5.7 8.6 %march.3 = (s32[2,256,128]{2,1,0:T(8,128)}, s32[2,256,128]{2,1,0:T(8,128)}, f32[2,128,128]{2,1,0:T(8,128)}) custom-call(f32[1,16]{1,0:T(1,128)} %bitcast.39, f32[1,16]{1,0:T(1,128)} %bitcast.42, f32[1,16]{1,0:T(1,128)} %bitcast.45, f32[3,16]{1,0:T(4,128)} %refs_3_.5, bf16[12,768,512]{2,1,0:T(8,128)(2,1)} %bitcast.29, bf16[1,128,512]{2,1,0:T(8,128)(2,1)} %pad.16.refs_5_, ...), custom_call_target="tpu_custom_call" | custom-call | flops 31457280 | bytes 1572864 | tf_op jit(solution)/shard_map/march/pallas_call | solution.py:271
  14.3 0.0 collective-permute-done
  14.4 0.1 pad_maximum_fusion.3
  14.5 0.7 fusion.2.refs_5_
  15.3 15.2 %march.4 = (s32[64,24,256]{2,1,0:T(8,128)}, f32[4,128,128]{2,1,0:T(8,128)}) custom-call(f32[1,16]{1,0:T(1,128)} %bitcast.40, f32[1,16]{1,0:T(1,128)} %bitcast.43, f32[1,16]{1,0:T(1,128)} %bitcast.46, f32[3,16]{1,0:T(4,128)} %refs_3_.5, bf16[12,768,512]{2,1,0:T(8,128)(2,1)} %bitcast.30, bf16[2,128,512]{2,1,0:T(8,128)(2,1)} %fusion.2.refs_5_, ...), custom_call_target="tpu_custom_call" | custom-call | flops 62914560 | bytes 3145728 | tf_op jit(solution)/shard_map/march/pallas_call | solution.py:271
  30.4 0.0 copy-start.3
  30.4 0.0 copy-start.4
  30.4 12.7 %all-to-all-start = ((s32[64,24,256]{2,1,0:T(8,128)}), s32[64,24,256]{2,1,0:T(8,128)S(1)}, u32[]{:S(2)}, u32[]{:S(2)}) async-start(s32[64,24,256]{2,1,0:T(8,128)} %get-tuple-element.14), calls=%async_computation | async-start | bytes 3145728 | tf_op jit(solution)/shard_map/all_to_all | solution.py:389
  43.2 0.0 copy-start
  43.2 0.0 copy-start.2
  43.2 0.0 copy-done.3
  43.3 0.0 copy-done.4
  43.3 0.0 copy-start.1
  43.3 0.1 fusion.10
  43.5 0.4 collective-permute-start.1
  43.9 0.3 copy-done
  44.2 0.0 copy-done.2
  44.2 0.8 pad_maximum_fusion.refs_6_
  45.0 1.5 %collective-permute-done.1 = bf16[12,768]{1,0:T(8,128)(2,1)S(1)} collective-permute-done((bf16[12,768]{1,0:T(8,128)(2,1)S(1)}, bf16[12,768]{1,0:T(8,128)(2,1)S(1)}, u32[]{:S(2)}, u32[]{:S(2)}) %collective-permute-start.1) | collective-permute-done | bytes 18464 | tf_op jit(solution)/shard_map/ppermute | solution.py:28
  46.5 0.6 pad_maximum_fusion.2.refs_8_
  47.2 0.0 copy-done.1
  47.2 17.8 %march.5 = s32[64,24,256]{2,1,0:T(8,128)} custom-call(f32[1,16]{1,0:T(1,128)} %bitcast.41, f32[1,16]{1,0:T(1,128)} %bitcast.44, f32[1,16]{1,0:T(1,128)} %bitcast.47, f32[3,16]{1,0:T(4,128)} %refs_3_.5, bf16[12,768,512]{2,1,0:T(8,128)(2,1)} %bitcast.31, bf16[12,768,512]{2,1,0:T(8,128)(2,1)} %bitcast.32, bf16[3,128,512]{2,1,0:T(8,128)(2,1)} %pad_maximum_fusion.refs_6_, ...), custom_call_target="tpu_custom_call" | custom-call | flops 94371840 | bytes 4718592 | tf_op jit(solution)/shard_map/march/pallas_call | solution.py:271
  65.0 17.2 %all-to-all-done.got_ref = s32[64,24,256]{2,1,0:T(8,128)S(1)} async-done(((s32[64,24,256]{2,1,0:T(8,128)}), s32[64,24,256]{2,1,0:T(8,128)S(1)}, u32[]{:S(2)}, u32[]{:S(2)}) %all-to-all-start) | async-done | bytes 1572896 | tf_op jit(solution)/shard_map/all_to_all | solution.py:389
  82.2 6.4 %all-to-all-start.1 = ((s32[64,24,256]{2,1,0:T(8,128)}), s32[64,24,256]{2,1,0:T(8,128)S(1)}, u32[]{:S(2)}, u32[]{:S(2)}) async-start(s32[64,24,256]{2,1,0:T(8,128)} %march.5), calls=%async_computation.1 | async-start | bytes 3145728 | tf_op jit(solution)/shard_map/all_to_all | solution.py:399
  88.6 2.9 %blend.2 = (f32[4,12,1,512]{3,2,1,0:T(1,128)}, s32[64]{0:T(128)}) custom-call(s32[64]{0:T(128)} %place_ref.1, s32[64,24,256]{2,1,0:T(8,128)S(1)} %all-to-all-done.got_ref), custom_call_target="tpu_custom_call" | custom-call | flops 15728640 | bytes 1572864 | tf_op jit(solution)/shard_map/blend/pallas_call | solution.py:353
  91.5 36.1 %all-to-all-done.1.got_ref = s32[64,24,256]{2,1,0:T(8,128)S(1)} async-done(((s32[64,24,256]{2,1,0:T(8,128)}), s32[64,24,256]{2,1,0:T(8,128)S(1)}, u32[]{:S(2)}, u32[]{:S(2)}) %all-to-all-start.1) | async-done | bytes 1572896 | tf_op jit(solution)/shard_map/all_to_all | solution.py:399
  127.7 2.5 %blend.3 = f32[4,12,1,512]{3,2,1,0:T(1,128)} custom-call(s32[64]{0:T(128)} %get-tuple-element.15.order_ref, s32[64,24,256]{2,1,0:T(8,128)S(1)} %all-to-all-done.1.got_ref, f32[4,12,1,512]{3,2,1,0:T(1,128)} %get-tuple-element.18.image_ref), custom_call_target="tpu_custom_call" | custom-call | flops 15728640 | bytes 1572864 | tf_op jit(solution)/shard_map/blend/pallas_call | solution.py:361
  (16 shorter events, 0.2 us)
Async XLA Ops:
  1.3 13.0 %collective-permute-start = (bf16[12,512]{1,0:T(8,128)(2,1)S(1)}, bf16[12,512]{1,0:T(8,128)(2,1)S(1)}, u32[]{:S(2)}, u32[]{:S(2)}) collective-permute-start(bf16[12,512]{1,0:T(8,128)(2,1)S(1)} %bitcast.38), channel_id=1, source_target_pairs={{0,2},{1,3},{2,0},{3,1},{4,6},{5,7},{6,4},{7,5},{8,10},{9,11},{10,... | collective-permute-start | bytes 36872 | tf_op jit(solution)/shard_map/ppermute | solution.py:28
  30.4 12.8 %copy-start.3 = (f32[4,128,128]{2,1,0:T(8,128)S(1)}, f32[4,128,128]{2,1,0:T(8,128)}, u32[]{:S(2)}) copy-start(f32[4,128,128]{2,1,0:T(8,128)} %get-tuple-element.16) | copy-start | bytes 786436
  30.4 12.8 %copy-start.4 = (f32[2,128,128]{2,1,0:T(8,128)S(1)}, f32[2,128,128]{2,1,0:T(8,128)}, u32[]{:S(2)}) copy-start(f32[2,128,128]{2,1,0:T(8,128)} %get-tuple-element.17) | copy-start | bytes 393220
  30.4 51.8 %all-to-all-start = ((s32[64,24,256]{2,1,0:T(8,128)}), s32[64,24,256]{2,1,0:T(8,128)S(1)}, u32[]{:S(2)}, u32[]{:S(2)}) async-start(s32[64,24,256]{2,1,0:T(8,128)} %get-tuple-element.14), calls=%async_computation | async-start | bytes 3145728 | tf_op jit(solution)/shard_map/all_to_all | solution.py:389
  43.2 1.0 copy-start
  43.2 1.0 copy-start.2
  43.3 3.9 %copy-start.1 = (f32[6,128,128]{2,1,0:T(8,128)}, f32[6,128,128]{2,1,0:T(8,128)S(1)}, u32[]{:S(2)}) copy-start(f32[6,128,128]{2,1,0:T(8,128)S(1)} %pad_maximum_fusion.1.refs_9_) | copy-start | bytes 1179652
  43.5 3.1 %collective-permute-start.1 = (bf16[12,768]{1,0:T(8,128)(2,1)S(1)}, bf16[12,768]{1,0:T(8,128)(2,1)S(1)}, u32[]{:S(2)}, u32[]{:S(2)}) collective-permute-start(bf16[12,768]{1,0:T(8,128)(2,1)S(1)} %bitcast.37), channel_id=1, source_target_pairs={{0,1},{1,0},{2,3},{3,2},{4,5},{5,4},{6,7},{7,6},{8,9},{9,8},{10,11... | collective-permute-start | bytes 55304 | tf_op jit(solution)/shard_map/ppermute | solution.py:28
  82.2 45.4 %all-to-all-start.1 = ((s32[64,24,256]{2,1,0:T(8,128)}), s32[64,24,256]{2,1,0:T(8,128)S(1)}, u32[]{:S(2)}, u32[]{:S(2)}) async-start(s32[64,24,256]{2,1,0:T(8,128)} %march.5), calls=%async_computation.1 | async-start | bytes 3145728 | tf_op jit(solution)/shard_map/all_to_all | solution.py:399
